TPU v7x, 32 devices: a whole 2x2x4 slice. The times are simulated.
32 devices in a mesh: groups: 2 (over x), tp: 8 (over z, y), sp: 2 (over core).
Axes of the slice: x: 2, y: 2, z: 4, core: 2. Of those that a mesh axis runs over, the one named last changes fastest.
Arguments:
- tokens: bfloat16 [1536, 4608], P(('groups', 'tp', 'sp')), parts along dimension 0, may hold values from -48 to 48
- w_query: bfloat16 [4608, 1024], P(None, 'tp'), may hold values from -0.09375 to 0.09375
- w_key: bfloat16 [4608, 512], P(None, 'tp'), may hold values from -0.09375 to 0.09375
- w_value: bfloat16 [4608, 512], P(None, 'tp'), may hold values from -0.09375 to 0.09375
- w_out: bfloat16 [1024, 4608], P('tp'), may hold values from -0.5 to 0.5
- doc_lengths: int32 [16], P('groups'), parts along dimension 0, may hold values from 1 to 192, 768 in all
Outputs:
- attn_out: bfloat16 [1536, 4608], P(('groups', 'tp', 'sp')), parts along dimension 0
There are 2 independent parts, one for each index of `groups`. A program takes and returns all parts, laid end to end along the dimension named above; an argument that names none is the same for every part. Nothing has to cross between parts.
Inputs may be any that keep to these rules, and one draw needn't show every extreme that they name: `doc_lengths`: positive lengths that sum to 768; the largest is exactly a quarter of 768.
All inputs are finite; a program needn't handle non-finite values.
Results may differ from a plain program's by a relative error of at most 0.024.
Values may be sent and summed in bfloat16 or wider, within the bound.
No kernel may reach another device: no remote copies, remote signals or barrier semaphores. Data moves between devices by JAX's collectives and lax.ppermute only.
A program may use at most 128 MiB of HBM per device.

v0:
```python
import jax
import jax.numpy as jnp
from jax import lax
from jax.experimental import pallas as pl
from jax.experimental.pallas import tpu as pltpu
from jax.sharding import PartitionSpec as P

PRE_SCALE = 144

masked_low = -1e30


def swap_tp(block, flip, only=None):
    count = lax.axis_size("tp")
    route = [(t, t ^ flip) for t in range(count) if only is None or only(t)]
    return lax.ppermute(block, "tp", route)


def swap_sp(block):
    count = lax.axis_size("sp")
    return lax.ppermute(block, "sp", [(s, s ^ 1) for s in range(count)])


def swap_in_slab(block, group_flip, tp_flip):
    groups = lax.axis_size("groups")
    count = lax.axis_size("tp")
    route = [
        (g * count + t, (g ^ group_flip) * count + (t ^ tp_flip))
        for g in range(groups)
        for t in range(count)
    ]
    return lax.ppermute(block, ("groups", "tp"), route)


def fence(*values):
    return lax.optimization_barrier(values)


def angles_of(places, head_dim):
    half_width = head_dim // 2
    spread = jnp.power(
        10000.0, -(jnp.arange(half_width, dtype=jnp.float32) * (2.0 / head_dim))
    )
    angles = places.astype(jnp.float32)[:, None] * spread[None, :]
    return jnp.cos(angles), jnp.sin(angles)


def rotate(matrix, cosine, sine_part):
    half_width = matrix.shape[1] // 2
    lower_part = matrix[:, :half_width]
    upper_part = matrix[:, half_width:]
    return jnp.concatenate(
        [
            lower_part * cosine - upper_part * sine_part,
            upper_part * cosine + lower_part * sine_part,
        ],
        axis=1,
    )


def doc_index(places, doc_ends):
    return jnp.sum((places[:, None] >= doc_ends[None, :]).astype(jnp.int32), axis=1)


def gather_first(block, slabs):
    if slabs != 4:
        return [swap_tp(block, 2 * k) for k in range(1, slabs)]
    return [swap_tp(block, 2), swap_tp(block, 4)]


def gather_last(block, came, slabs):
    if slabs != 4:
        return ()
    inner = lambda t: (t >> 1) in (1, 2)
    relayed = swap_tp(came[1], 2, inner)
    return (swap_tp(block, 6, inner), relayed)


def pick_last(last, slab):
    return [jnp.where((slab == 1) | (slab == 2), last[0], last[1])] if last else []


def project_kernel(peers, *refs):
    stacked, pieces, outs = refs[:peers], refs[peers:-peers], refs[-peers:]
    depth = pieces[0].shape[0]
    total = None
    for i, piece in enumerate(pieces):
        rows = jnp.concatenate([m[:, i * depth : (i + 1) * depth] for m in stacked], axis=0)
        term = jnp.dot(rows, piece[...], preferred_element_type=jnp.float32)
        total = term if total is None else total + term
    count = stacked[0].shape[0]
    for i, out in enumerate(outs):
        out[...] = total[i * count : (i + 1) * count].astype(out.dtype)


def project(stacked, pieces):
    rows, _ = stacked[0].shape
    _, width = pieces[0].shape
    peers = len(stacked)
    whole = pl.BlockSpec(memory_space=pltpu.VMEM)
    return pl.pallas_call(
        lambda *refs: project_kernel(peers, *refs),
        in_specs=[whole] * (peers + len(pieces)),
        out_specs=[whole] * peers,
        out_shape=[jax.ShapeDtypeStruct((rows, width), jnp.bfloat16)] * peers,
        name="project",
    )(*stacked, *pieces)


def local(tokens, w_query, w_key, w_value, w_out, doc_lengths):
    rows, width = tokens.shape
    tp_count = lax.axis_size("tp")
    sp_count = lax.axis_size("sp")
    sp_place = lax.axis_index("sp")
    tp_place = lax.axis_index("tp")
    slabs = tp_count // 2
    slab = tp_place // 2
    side = tp_place % 2
    head_dim = w_query.shape[1]
    half_dim = w_key.shape[1]

    depth = width // sp_count
    quarter = w_out.shape[1] // 4
    mine = (lax.axis_index("groups") % 2) * 2 + side
    wkv_own = jnp.concatenate([w_key.T, w_value.T], axis=0)
    share_q = lax.dynamic_slice_in_dim(w_query, sp_place * depth, depth, 0)
    share_kv = lax.dynamic_slice_in_dim(wkv_own, sp_place * depth, depth, 1)
    out_sent = lax.dynamic_slice_in_dim(w_out, (mine ^ 1) * quarter, quarter, 1)
    share_q, share_kv, out_sent, tokens, doc_lengths = fence(
        share_q, share_kv, out_sent, tokens, doc_lengths
    )
    came = gather_first(tokens, slabs)
    route = [
        ((t * sp_count + s), ((t ^ 1) * sp_count + s))
        for t in range(tp_count)
        for s in range(sp_count)
        if s == t % 2
    ]
    out_came = lax.ppermute(out_sent, ("tp", "sp"), route)
    came_q = swap_tp(share_q, 1)
    came_kv = swap_tp(share_kv, 1)
    other_q = swap_sp(came_q)
    other_kv = swap_sp(came_kv)
    ordered = lambda a, b, axis: jnp.concatenate(
        [jnp.where(sp_place == 0, a, b), jnp.where(sp_place == 0, b, a)], axis=axis
    )
    wq_pair = ordered(came_q, other_q, 0)
    wkv_pair = ordered(came_kv, other_kv, 1)
    out_kept = lax.dynamic_slice_in_dim(w_out, mine * quarter, quarter, 1)
    out_head = jnp.where(side == sp_place, out_kept, out_came)

    if slabs == 4:
        again, came[1] = fence(tokens, came[1])
        last = gather_last(again, came, slabs)
    else:
        last = ()
    blocks = [tokens] + came + pick_last(last, slab)
    out_first = gather_first(out_head, slabs)

    plain = lambda a, w: jnp.dot(a, w, preferred_element_type=jnp.float32)
    turned = lambda a, w: jnp.einsum("rk,ck->rc", a, w, preferred_element_type=jnp.float32)
    head = jnp.concatenate([tokens] + came, axis=0)
    tail = blocks[1 + len(came) :]

    def over(product, weight):
        results = [product(block, weight) for block in [head] + tail]
        return jnp.concatenate(results, axis=0) if tail else results[0]

    own_q, own_kv = over(plain, w_query), over(turned, wkv_own)
    pair_q, pair_kv = over(plain, wq_pair), over(turned, wkv_pair)

    doc_ends = jnp.cumsum(doc_lengths)
    row_ids = jnp.arange(rows, dtype=jnp.int32)
    slab_ids = slab ^ jnp.arange(slabs, dtype=jnp.int32)

    def places_of(at_side, at_sp):
        starts = ((slab_ids * 2 + at_side) * sp_count + at_sp) * rows
        return (starts[:, None] + row_ids[None, :]).reshape(-1)

    places = places_of(side, sp_place)
    cosine, sine_part = angles_of(places, head_dim)

    def half(lo, hi):
        return jnp.where(
            side == 0,
            jnp.concatenate([own_kv[:, lo:hi], pair_kv[:, lo:hi]], axis=1),
            jnp.concatenate([pair_kv[:, lo:hi], own_kv[:, lo:hi]], axis=1),
        ).astype(jnp.bfloat16)

    key_raw = half(0, half_dim)
    value_rows = half(half_dim, 2 * half_dim)
    key_rows = rotate(key_raw.astype(jnp.float32), cosine, sine_part).astype(jnp.bfloat16)
    queries = jnp.concatenate(
        [rotate(own_q, cosine, sine_part), rotate(pair_q, cosine, sine_part)], axis=0
    )
    queries = (queries * PRE_SCALE ** (-0.5)).astype(jnp.bfloat16)

    key_value = jnp.concatenate([key_rows, value_rows], axis=1)
    both = jnp.concatenate([key_value, swap_tp(key_value, 1)], axis=0)
    every = lax.all_gather(both, "sp", axis=0, tiled=True)
    key_places = jnp.concatenate(
        [places_of(b, s) for s in range(sp_count) for b in (side, 1 - side)]
    )
    key_docs = doc_index(key_places, doc_ends)
    query_docs = doc_index(places, doc_ends)
    allowed = (key_places[None, :] <= places[:, None]) & (key_docs[None, :] == query_docs[:, None])
    allowed = jnp.concatenate([allowed, allowed], axis=0)
    scores = jnp.einsum(
        "qd,kd->qk", queries, every[:, :head_dim], preferred_element_type=jnp.float32
    )
    largest = jnp.max(jnp.where(allowed, scores, masked_low), axis=1, keepdims=True)
    weights = jnp.where(allowed, jnp.exp(scores - largest), 0.0)
    denominator = jnp.sum(weights, axis=1, keepdims=True)
    mixed = jnp.dot(
        weights.astype(jnp.bfloat16), every[:, head_dim:], preferred_element_type=jnp.float32
    )
    mixed = (mixed / denominator).astype(jnp.bfloat16)
    count = slabs * rows
    lower, upper = mixed[:count], mixed[count:]
    straight = side == sp_place
    mixed = jnp.concatenate(
        [jnp.where(straight, lower, upper), jnp.where(straight, upper, lower)], axis=1
    )
    parts = [mixed[:rows]]
    for k in range(1, slabs):
        parts.append(swap_tp(mixed[k * rows : (k + 1) * rows], 2 * k))
    out_last = gather_last(out_head, out_first, slabs)
    merged = jnp.concatenate(parts, axis=1)
    peers = ((0, 0), (1, 0), (0, 1), (1, 1))
    stacked = [merged] + [swap_in_slab(merged, g, t) for g, t in peers[1:]]
    if slabs == 4:
        *out_last, stacked[1] = fence(*out_last, stacked[1])
    out_pieces = []
    for piece in [out_head] + out_first + pick_last(out_last, slab):
        out_pieces += [piece, swap_sp(piece)]
    outs = project(stacked, out_pieces)
    outs = [outs[0]] + [swap_in_slab(o, g, t) for o, (g, t) in zip(outs[1:], peers[1:])]
    swap_y = side == 1
    swap_x = lax.axis_index("groups") % 2 == 1
    rows_of = lambda a, b: (jnp.where(swap_y, b, a), jnp.where(swap_y, a, b))
    near = rows_of(outs[0], outs[2])
    far = rows_of(outs[1], outs[3])
    return jnp.concatenate(
        [jnp.where(swap_x, f, n) for n, f in zip(near, far)]
        + [jnp.where(swap_x, n, f) for n, f in zip(near, far)],
        axis=1,
    )


def solution(mesh):
    placed = (
        P(("groups", "tp", "sp"), None),
        P(None, "tp"),
        P(None, "tp"),
        P(None, "tp"),
        P("tp", None),
        P("groups"),
    )

    return jax.shard_map(
        local,
        mesh=mesh,
        in_specs=placed,
        out_specs=P(("groups", "tp", "sp"), None),
        check_vma=False,
    )
```

profile of v0, /device:TPU:0, one launch (start us, length us, event | category | flops | bytes accessed | tf_op | source)
XLA Modules:
  0.0 115.0 jit_solution(7666755856293874544)
XLA Ops:
  3.1 3.1 %collective-permute-start = (bf16[48,4608]{1,0:T(8,128)(2,1)}, bf16[48,4608]{1,0:T(8,128)(2,1)}, u32[]{:S(2)}, u32[]{:S(2)}) collective-permute-start(bf16[48,4608]{1,0:T(8,128)(2,1)} %param.6), channel_id=1, source_target_pairs={{0,4},{2,6},{4,0},{6,2},{8,12},{10,14},{12,8},{14,10},{1,5},{3,7},... | collective-permute-start | bytes 1327112 | tf_op jit(solution)/shard_map/ppermute | solution.py:16
  6.2 2.6 %collective-permute-start.1 = (bf16[48,4608]{1,0:T(8,128)(2,1)}, bf16[48,4608]{1,0:T(8,128)(2,1)}, u32[]{:S(2)}, u32[]{:S(2)}) collective-permute-start(bf16[48,4608]{1,0:T(8,128)(2,1)} %param.6), channel_id=1, source_target_pairs={{0,8},{2,10},{4,12},{6,14},{8,0},{10,2},{12,4},{14,6},{1,9},{3,11}... | collective-permute-start | bytes 1327112 | tf_op jit(solution)/shard_map/ppermute | solution.py:16
  8.8 1.5 %collective-permute-start.4 = (bf16[2304,128]{1,0:T(8,128)(2,1)}, bf16[2304,128]{1,0:T(8,128)(2,1)}, u32[]{:S(2)}, u32[]{:S(2)}) collective-permute-start(bf16[2304,128]{1,0:T(8,128)(2,1)} %constant_dynamic-slice_fusion.1), channel_id=1, source_target_pairs={{0,2},{2,0},{4,6},{6,4},{8,10},{10,8},{12,14},{14,12},{1,3},{3,1},... | collective-permute-start | bytes 1769480 | tf_op jit(solution)/shard_map/ppermute | solution.py:16
  10.8 4.1 %collective-permute-start.12 = (bf16[128,1152]{1,0:T(8,128)(2,1)S(1)}, bf16[128,1152]{1,0:T(8,128)(2,1)}, u32[]{:S(2)}, u32[]{:S(2)}) collective-permute-start(bf16[128,1152]{1,0:T(8,128)(2,1)S(1)} %constant_dynamic-slice_fusion), channel_id=1, source_target_pairs={{0,2},{3,1},{4,6},{7,5},{8,10},{11,9},{12,14},{15,13},{16,18},{19,... | collective-permute-start | bytes 884744 | tf_op jit(solution)/shard_map/ppermute | solution.py:139
  17.5 20.8 %collective-permute-done.12 = bf16[128,1152]{1,0:T(8,128)(2,1)} collective-permute-done((bf16[128,1152]{1,0:T(8,128)(2,1)S(1)}, bf16[128,1152]{1,0:T(8,128)(2,1)}, u32[]{:S(2)}, u32[]{:S(2)}) %collective-permute-start.12) | collective-permute-done | bytes 294944 | tf_op jit(solution)/shard_map/ppermute | solution.py:139
  39.8 1.3 %collective-permute-start.3 = (bf16[48,4608]{1,0:T(8,128)(2,1)}, bf16[48,4608]{1,0:T(8,128)(2,1)S(1)}, u32[]{:S(2)}, u32[]{:S(2)}) collective-permute-start(bf16[48,4608]{1,0:T(8,128)(2,1)} %collective-permute-done.1), channel_id=1, source_target_pairs={{4,0},{6,2},{8,12},{10,14},{5,1},{7,3},{9,13},{11,15},{20,16},{22,... | collective-permute-start | bytes 1327112 | tf_op jit(solution)/shard_map/ppermute | solution.py:16
  45.6 7.2 %collective-permute-start.20 = (bf16[128,1152]{1,0:T(8,128)(2,1)S(1)}, bf16[128,1152]{1,0:T(8,128)(2,1)S(1)}, u32[]{:S(2)}, u32[]{:S(2)}) collective-permute-start(bf16[128,1152]{1,0:T(8,128)(2,1)S(1)} %dynamic-slice_select_fusion.refs_4_), channel_id=1, source_target_pairs={{0,4},{2,6},{4,0},{6,2},{8,12},{10,14},{12,8},{14,10},{1,5},{3,7},... | collective-permute-start | bytes 884744 | tf_op jit(solution)/shard_map/ppermute | solution.py:16
  52.8 3.7 %collective-permute-done.14.refs_8_ = bf16[128,1152]{1,0:T(8,128)(2,1)S(1)} collective-permute-done((bf16[128,1152]{1,0:T(8,128)(2,1)S(1)}, bf16[128,1152]{1,0:T(8,128)(2,1)S(1)}, u32[]{:S(2)}, u32[]{:S(2)}) %collective-permute-start.14) | collective-permute-done | bytes 294944 | tf_op jit(solution)/shard_map/ppermute | solution.py:16
  57.0 4.1 %collective-permute-done.3 = bf16[48,4608]{1,0:T(8,128)(2,1)S(1)} collective-permute-done((bf16[48,4608]{1,0:T(8,128)(2,1)}, bf16[48,4608]{1,0:T(8,128)(2,1)S(1)}, u32[]{:S(2)}, u32[]{:S(2)}) %collective-permute-start.3) | collective-permute-done | bytes 442400 | tf_op jit(solution)/shard_map/ppermute | solution.py:16
  67.3 2.6 %collective-permute-start.8 = (bf16[192,256]{1,0:T(8,128)(2,1)S(1)}, bf16[192,256]{1,0:T(8,128)(2,1)S(1)}, u32[]{:S(2)}, u32[]{:S(2)}) collective-permute-start(bf16[192,256]{1,0:T(8,128)(2,1)S(1)} %pad_maximum_fusion.15), channel_id=1, source_target_pairs={{0,2},{2,0},{4,6},{6,4},{8,10},{10,8},{12,14},{14,12},{1,3},{3,1},... | collective-permute-start | bytes 294920 | tf_op jit(solution)/shard_map/ppermute | solution.py:16
  70.3 2.1 %collective-permute-done.8 = bf16[192,256]{1,0:T(8,128)(2,1)S(1)} collective-permute-done((bf16[192,256]{1,0:T(8,128)(2,1)S(1)}, bf16[192,256]{1,0:T(8,128)(2,1)S(1)}, u32[]{:S(2)}, u32[]{:S(2)}) %collective-permute-start.8) | collective-permute-done | bytes 98336 | tf_op jit(solution)/shard_map/ppermute | solution.py:16
  72.6 2.1 %all_gather.3 = bf16[768,256]{1,0:T(8,128)(2,1)S(1)} all-gather(bf16[384,256]{1,0:T(8,128)(2,1)S(1)} %pad_maximum_fusion.10), channel_id=1, replica_groups=mesh['groups'=2,'tp'=8,'sp'=2] {'sp'}, dimensions={0}, use_global_device_ids=true | all-gather | bytes 589824 | tf_op jit(solution)/shard_map/all_gather | solution.py:200
  76.0 4.6 %collective-permute-start.10 = (bf16[48,256]{1,0:T(8,128)(2,1)S(1)}, bf16[48,256]{1,0:T(8,128)(2,1)S(1)}, u32[]{:S(2)}, u32[]{:S(2)}) collective-permute-start(bf16[48,256]{1,0:T(8,128)(2,1)S(1)} %get-tuple-element.50), channel_id=1, source_target_pairs={{0,8},{2,10},{4,12},{6,14},{8,0},{10,2},{12,4},{14,6},{1,9},{3,11}... | collective-permute-start | bytes 73736 | tf_op jit(solution)/shard_map/ppermute | solution.py:16
  80.7 3.3 %collective-permute-start.11 = (bf16[48,256]{1,0:T(8,128)(2,1)S(1)}, bf16[48,256]{1,0:T(8,128)(2,1)S(1)}, u32[]{:S(2)}, u32[]{:S(2)}) collective-permute-start(bf16[48,256]{1,0:T(8,128)(2,1)S(1)} %get-tuple-element.49), channel_id=1, source_target_pairs={{0,12},{2,14},{4,8},{6,10},{8,4},{10,6},{12,0},{14,2},{1,13},{3,15... | collective-permute-start | bytes 73736 | tf_op jit(solution)/shard_map/ppermute | solution.py:16
  83.9 2.4 %collective-permute-start.9 = (bf16[48,256]{1,0:T(8,128)(2,1)S(1)}, bf16[48,256]{1,0:T(8,128)(2,1)S(1)}, u32[]{:S(2)}, u32[]{:S(2)}) collective-permute-start(bf16[48,256]{1,0:T(8,128)(2,1)S(1)} %get-tuple-element.48), channel_id=1, source_target_pairs={{0,4},{2,6},{4,0},{6,2},{8,12},{10,14},{12,8},{14,10},{1,5},{3,7},... | collective-permute-start | bytes 73736 | tf_op jit(solution)/shard_map/ppermute | solution.py:16
  86.3 1.8 %collective-permute-done.9 = bf16[48,256]{1,0:T(8,128)(2,1)S(1)} collective-permute-done((bf16[48,256]{1,0:T(8,128)(2,1)S(1)}, bf16[48,256]{1,0:T(8,128)(2,1)S(1)}, u32[]{:S(2)}, u32[]{:S(2)}) %collective-permute-start.9) | collective-permute-done | bytes 24608 | tf_op jit(solution)/shard_map/ppermute | solution.py:16
  88.1 1.6 %collective-permute-start.16 = (bf16[48,1024]{1,0:T(8,128)(2,1)S(1)}, bf16[48,1024]{1,0:T(8,128)(2,1)S(1)}, u32[]{:S(2)}, u32[]{:S(2)}) collective-permute-start(bf16[48,1024]{1,0:T(8,128)(2,1)S(1)} %pad_maximum_fusion.16.refs_0_), channel_id=1, source_target_pairs={{0,16},{2,18},{4,20},{6,22},{8,24},{10,26},{12,28},{14,30},{16,0},... | collective-permute-start | bytes 294920 | tf_op jit(solution)/shard_map/ppermute | solution.py:32
  90.3 2.5 %collective-permute-done.16.refs_1_ = bf16[48,1024]{1,0:T(8,128)(2,1)S(1)} collective-permute-done((bf16[48,1024]{1,0:T(8,128)(2,1)S(1)}, bf16[48,1024]{1,0:T(8,128)(2,1)S(1)}, u32[]{:S(2)}, u32[]{:S(2)}) %collective-permute-start.16) | collective-permute-done | bytes 98336 | tf_op jit(solution)/shard_map/ppermute | solution.py:32
  93.3 2.7 %collective-permute-start.18 = (bf16[48,1024]{1,0:T(8,128)(2,1)S(1)}, bf16[48,1024]{1,0:T(8,128)(2,1)S(1)}, u32[]{:S(2)}, u32[]{:S(2)}) collective-permute-start(bf16[48,1024]{1,0:T(8,128)(2,1)S(1)} %pad_maximum_fusion.16.refs_0_), channel_id=1, source_target_pairs={{0,18},{2,16},{4,22},{6,20},{8,26},{10,24},{12,30},{14,28},{16,2},... | collective-permute-start | bytes 294920 | tf_op jit(solution)/shard_map/ppermute | solution.py:32
  96.0 4.3 %collective-permute-done.17.refs_2_ = bf16[48,1024]{1,0:T(8,128)(2,1)S(1)} collective-permute-done((bf16[48,1024]{1,0:T(8,128)(2,1)S(1)}, bf16[48,1024]{1,0:T(8,128)(2,1)S(1)}, u32[]{:S(2)}, u32[]{:S(2)}) %collective-permute-start.17) | collective-permute-done | bytes 98336 | tf_op jit(solution)/shard_map/ppermute | solution.py:32
  101.6 3.6 %project.1 = (bf16[48,1152]{1,0:T(8,128)(2,1)}, bf16[48,1152]{1,0:T(8,128)(2,1)}, bf16[48,1152]{1,0:T(8,128)(2,1)}, bf16[48,1152]{1,0:T(8,128)(2,1)}) custom-call(bf16[48,1024]{1,0:T(8,128)(2,1)} %copy-done.7, bf16[48,1024]{1,0:T(8,128)(2,1)} %copy-done.14, bf16[48,1024]{1,0:T(8,128)(2,1)} %copy-done.15, bf16[48,1024]{1,0:T(8,128)(2,1)} %copy-done.16, ...), custom_call_target="tpu_custom_call" | custom-call | tf_op jit(solution)/shard_map/project/pallas_call | solution.py:101
  105.2 1.4 %collective-permute-start.24 = (bf16[48,1152]{1,0:T(8,128)(2,1)}, bf16[48,1152]{1,0:T(8,128)(2,1)S(1)}, u32[]{:S(2)}, u32[]{:S(2)}) collective-permute-start(bf16[48,1152]{1,0:T(8,128)(2,1)} %get-tuple-element.29), channel_id=1, source_target_pairs={{0,18},{2,16},{4,22},{6,20},{8,26},{10,24},{12,30},{14,28},{16,2},... | collective-permute-start | bytes 331784 | tf_op jit(solution)/shard_map/ppermute | solution.py:32
  107.2 1.5 %collective-permute-start.26 = (bf16[48,1152]{1,0:T(8,128)(2,1)}, bf16[48,1152]{1,0:T(8,128)(2,1)S(1)}, u32[]{:S(2)}, u32[]{:S(2)}) collective-permute-start(bf16[48,1152]{1,0:T(8,128)(2,1)} %get-tuple-element.31), channel_id=1, source_target_pairs={{0,2},{2,0},{4,6},{6,4},{8,10},{10,8},{12,14},{14,12},{16,18},{18,... | collective-permute-start | bytes 331784 | tf_op jit(solution)/shard_map/ppermute | solution.py:32
  108.7 3.4 %collective-permute-done.24 = bf16[48,1152]{1,0:T(8,128)(2,1)S(1)} collective-permute-done((bf16[48,1152]{1,0:T(8,128)(2,1)}, bf16[48,1152]{1,0:T(8,128)(2,1)S(1)}, u32[]{:S(2)}, u32[]{:S(2)}) %collective-permute-start.24) | collective-permute-done | bytes 110624 | tf_op jit(solution)/shard_map/ppermute | solution.py:32
  (122 shorter events, 26.3 us)
Async XLA Ops:
  3.1 37.9 %collective-permute-start = (bf16[48,4608]{1,0:T(8,128)(2,1)}, bf16[48,4608]{1,0:T(8,128)(2,1)}, u32[]{:S(2)}, u32[]{:S(2)}) collective-permute-start(bf16[48,4608]{1,0:T(8,128)(2,1)} %param.6), channel_id=1, source_target_pairs={{0,4},{2,6},{4,0},{6,2},{8,12},{10,14},{12,8},{14,10},{1,5},{3,7},... | collective-permute-start | bytes 1327112 | tf_op jit(solution)/shard_map/ppermute | solution.py:16
  6.2 33.6 %collective-permute-start.1 = (bf16[48,4608]{1,0:T(8,128)(2,1)}, bf16[48,4608]{1,0:T(8,128)(2,1)}, u32[]{:S(2)}, u32[]{:S(2)}) collective-permute-start(bf16[48,4608]{1,0:T(8,128)(2,1)} %param.6), channel_id=1, source_target_pairs={{0,8},{2,10},{4,12},{6,14},{8,0},{10,2},{12,4},{14,6},{1,9},{3,11}... | collective-permute-start | bytes 1327112 | tf_op jit(solution)/shard_map/ppermute | solution.py:16
  8.8 36.1 %collective-permute-start.4 = (bf16[2304,128]{1,0:T(8,128)(2,1)}, bf16[2304,128]{1,0:T(8,128)(2,1)}, u32[]{:S(2)}, u32[]{:S(2)}) collective-permute-start(bf16[2304,128]{1,0:T(8,128)(2,1)} %constant_dynamic-slice_fusion.1), channel_id=1, source_target_pairs={{0,2},{2,0},{4,6},{6,4},{8,10},{10,8},{12,14},{14,12},{1,3},{3,1},... | collective-permute-start | bytes 1769480 | tf_op jit(solution)/shard_map/ppermute | solution.py:16
  10.3 35.3 %collective-permute-start.6 = (bf16[128,2304]{1,0:T(8,128)(2,1)}, bf16[128,2304]{1,0:T(8,128)(2,1)S(1)}, u32[]{:S(2)}, u32[]{:S(2)}) collective-permute-start(bf16[128,2304]{1,0:T(8,128)(2,1)} %fusion.10), channel_id=1, source_target_pairs={{0,2},{2,0},{4,6},{6,4},{8,10},{10,8},{12,14},{14,12},{1,3},{3,1},... | collective-permute-start | bytes 1769480 | tf_op jit(solution)/shard_map/ppermute | solution.py:16
  10.8 27.5 %collective-permute-start.12 = (bf16[128,1152]{1,0:T(8,128)(2,1)S(1)}, bf16[128,1152]{1,0:T(8,128)(2,1)}, u32[]{:S(2)}, u32[]{:S(2)}) collective-permute-start(bf16[128,1152]{1,0:T(8,128)(2,1)S(1)} %constant_dynamic-slice_fusion), channel_id=1, source_target_pairs={{0,2},{3,1},{4,6},{7,5},{8,10},{11,9},{12,14},{15,13},{16,18},{19,... | collective-permute-start | bytes 884744 | tf_op jit(solution)/shard_map/ppermute | solution.py:139
  39.4 17.1 %collective-permute-start.14 = (bf16[128,1152]{1,0:T(8,128)(2,1)S(1)}, bf16[128,1152]{1,0:T(8,128)(2,1)S(1)}, u32[]{:S(2)}, u32[]{:S(2)}) collective-permute-start(bf16[128,1152]{1,0:T(8,128)(2,1)S(1)} %dynamic-slice_select_fusion.refs_4_), channel_id=1, source_target_pairs={{0,8},{2,10},{4,12},{6,14},{8,0},{10,2},{12,4},{14,6},{1,9},{3,11}... | collective-permute-start | bytes 884744 | tf_op jit(solution)/shard_map/ppermute | solution.py:16
  39.8 21.4 %collective-permute-start.3 = (bf16[48,4608]{1,0:T(8,128)(2,1)}, bf16[48,4608]{1,0:T(8,128)(2,1)S(1)}, u32[]{:S(2)}, u32[]{:S(2)}) collective-permute-start(bf16[48,4608]{1,0:T(8,128)(2,1)} %collective-permute-done.1), channel_id=1, source_target_pairs={{4,0},{6,2},{8,12},{10,14},{5,1},{7,3},{9,13},{11,15},{20,16},{22,... | collective-permute-start | bytes 1327112 | tf_op jit(solution)/shard_map/ppermute | solution.py:16
  43.2 13.4 %collective-permute-start.2 = (bf16[48,4608]{1,0:T(8,128)(2,1)}, bf16[48,4608]{1,0:T(8,128)(2,1)S(1)}, u32[]{:S(2)}, u32[]{:S(2)}) collective-permute-start(bf16[48,4608]{1,0:T(8,128)(2,1)} %param.6), channel_id=1, source_target_pairs={{4,8},{6,10},{8,4},{10,6},{5,9},{7,11},{9,5},{11,7},{20,24},{22,26... | collective-permute-start | bytes 1327112 | tf_op jit(solution)/shard_map/ppermute | solution.py:16
  44.9 44.8 %collective-permute-start.13 = (bf16[128,1152]{1,0:T(8,128)(2,1)S(1)}, bf16[128,1152]{1,0:T(8,128)(2,1)S(1)}, u32[]{:S(2)}, u32[]{:S(2)}) collective-permute-start(bf16[128,1152]{1,0:T(8,128)(2,1)S(1)} %dynamic-slice_select_fusion.refs_4_), channel_id=1, source_target_pairs={{4,8},{6,10},{8,4},{10,6},{5,9},{7,11},{9,5},{11,7},{20,24},{22,26... | collective-permute-start | bytes 884744 | tf_op jit(solution)/shard_map/ppermute | solution.py:16
  45.6 44.6 %collective-permute-start.20 = (bf16[128,1152]{1,0:T(8,128)(2,1)S(1)}, bf16[128,1152]{1,0:T(8,128)(2,1)S(1)}, u32[]{:S(2)}, u32[]{:S(2)}) collective-permute-start(bf16[128,1152]{1,0:T(8,128)(2,1)S(1)} %dynamic-slice_select_fusion.refs_4_), channel_id=1, source_target_pairs={{0,4},{2,6},{4,0},{6,2},{8,12},{10,14},{12,8},{14,10},{1,5},{3,7},... | collective-permute-start | bytes 884744 | tf_op jit(solution)/shard_map/ppermute | solution.py:16
  56.5 6.9 %collective-permute-start.5 = (bf16[2304,128]{1,0:T(8,128)(2,1)}, bf16[2304,128]{1,0:T(8,128)(2,1)S(1)}, u32[]{:S(2)}, u32[]{:S(2)}) collective-permute-start(bf16[2304,128]{1,0:T(8,128)(2,1)} %collective-permute-done.4), channel_id=1, source_target_pairs={{0,1},{1,0},{2,3},{3,2},{4,5},{5,4},{6,7},{7,6},{8,9},{9,8},{10,11... | collective-permute-start | bytes 1769480 | tf_op jit(solution)/shard_map/ppermute | solution.py:21
  56.6 8.8 %collective-permute-start.7 = (bf16[128,2304]{1,0:T(8,128)(2,1)S(1)}, bf16[128,2304]{1,0:T(8,128)(2,1)S(1)}, u32[]{:S(2)}, u32[]{:S(2)}) collective-permute-start(bf16[128,2304]{1,0:T(8,128)(2,1)S(1)} %collective-permute-done.6), channel_id=1, source_target_pairs={{0,1},{1,0},{2,3},{3,2},{4,5},{5,4},{6,7},{7,6},{8,9},{9,8},{10,11... | collective-permute-start | bytes 1769480 | tf_op jit(solution)/shard_map/ppermute | solution.py:21
  61.1 29.2 %collective-permute-start.15 = (bf16[128,1152]{1,0:T(8,128)(2,1)S(1)}, bf16[128,1152]{1,0:T(8,128)(2,1)S(1)}, u32[]{:S(2)}, u32[]{:S(2)}) collective-permute-start(bf16[128,1152]{1,0:T(8,128)(2,1)S(1)} %collective-permute-done.14.refs_8_), channel_id=1, source_target_pairs={{4,0},{6,2},{8,12},{10,14},{5,1},{7,3},{9,13},{11,15},{20,16},{22,... | collective-permute-start | bytes 884744 | tf_op jit(solution)/shard_map/ppermute | solution.py:16
  67.3 5.2 %collective-permute-start.8 = (bf16[192,256]{1,0:T(8,128)(2,1)S(1)}, bf16[192,256]{1,0:T(8,128)(2,1)S(1)}, u32[]{:S(2)}, u32[]{:S(2)}) collective-permute-start(bf16[192,256]{1,0:T(8,128)(2,1)S(1)} %pad_maximum_fusion.15), channel_id=1, source_target_pairs={{0,2},{2,0},{4,6},{6,4},{8,10},{10,8},{12,14},{14,12},{1,3},{3,1},... | collective-permute-start | bytes 294920 | tf_op jit(solution)/shard_map/ppermute | solution.py:16
  76.0 7.9 %collective-permute-start.10 = (bf16[48,256]{1,0:T(8,128)(2,1)S(1)}, bf16[48,256]{1,0:T(8,128)(2,1)S(1)}, u32[]{:S(2)}, u32[]{:S(2)}) collective-permute-start(bf16[48,256]{1,0:T(8,128)(2,1)S(1)} %get-tuple-element.50), channel_id=1, source_target_pairs={{0,8},{2,10},{4,12},{6,14},{8,0},{10,2},{12,4},{14,6},{1,9},{3,11}... | collective-permute-start | bytes 73736 | tf_op jit(solution)/shard_map/ppermute | solution.py:16
  80.7 5.6 %collective-permute-start.11 = (bf16[48,256]{1,0:T(8,128)(2,1)S(1)}, bf16[48,256]{1,0:T(8,128)(2,1)S(1)}, u32[]{:S(2)}, u32[]{:S(2)}) collective-permute-start(bf16[48,256]{1,0:T(8,128)(2,1)S(1)} %get-tuple-element.49), channel_id=1, source_target_pairs={{0,12},{2,14},{4,8},{6,10},{8,4},{10,6},{12,0},{14,2},{1,13},{3,15... | collective-permute-start | bytes 73736 | tf_op jit(solution)/shard_map/ppermute | solution.py:16
  89.7 6.3 %collective-permute-start.22 = (bf16[128,1152]{1,0:T(8,128)(2,1)S(1)}, bf16[128,1152]{1,0:T(8,128)(2,1)S(1)}, u32[]{:S(2)}, u32[]{:S(2)}) collective-permute-start(bf16[128,1152]{1,0:T(8,128)(2,1)S(1)} %collective-permute-done.14.refs_8_), channel_id=1, source_target_pairs={{0,1},{1,0},{2,3},{3,2},{4,5},{5,4},{6,7},{7,6},{8,9},{9,8},{10,11... | collective-permute-start | bytes 884744 | tf_op jit(solution)/shard_map/ppermute | solution.py:21
  90.2 5.8 %collective-permute-start.21 = (bf16[128,1152]{1,0:T(8,128)(2,1)S(1)}, bf16[128,1152]{1,0:T(8,128)(2,1)S(1)}, u32[]{:S(2)}, u32[]{:S(2)}) collective-permute-start(bf16[128,1152]{1,0:T(8,128)(2,1)S(1)} %collective-permute-done.20.refs_6_), channel_id=1, source_target_pairs={{0,1},{1,0},{2,3},{3,2},{4,5},{5,4},{6,7},{7,6},{8,9},{9,8},{10,11... | collective-permute-start | bytes 884744 | tf_op jit(solution)/shard_map/ppermute | solution.py:21
  92.9 7.4 %collective-permute-start.23 = (bf16[128,1152]{1,0:T(8,128)(2,1)S(1)}, bf16[128,1152]{1,0:T(8,128)(2,1)S(1)}, u32[]{:S(2)}, u32[]{:S(2)}) collective-permute-start(bf16[128,1152]{1,0:T(8,128)(2,1)S(1)} %broadcast_select_fusion.5.refs_10_), channel_id=1, source_target_pairs={{0,1},{1,0},{2,3},{3,2},{4,5},{5,4},{6,7},{7,6},{8,9},{9,8},{10,11... | collective-permute-start | bytes 884744 | tf_op jit(solution)/shard_map/ppermute | solution.py:21
  92.9 7.3 %collective-permute-start.17 = (bf16[48,1024]{1,0:T(8,128)(2,1)S(1)}, bf16[48,1024]{1,0:T(8,128)(2,1)S(1)}, u32[]{:S(2)}, u32[]{:S(2)}) collective-permute-start(bf16[48,1024]{1,0:T(8,128)(2,1)S(1)} %pad_maximum_fusion.16.refs_0_), channel_id=1, source_target_pairs={{0,2},{2,0},{4,6},{6,4},{8,10},{10,8},{12,14},{14,12},{16,18},{18,... | collective-permute-start | bytes 294920 | tf_op jit(solution)/shard_map/ppermute | solution.py:32
  93.3 7.0 %collective-permute-start.18 = (bf16[48,1024]{1,0:T(8,128)(2,1)S(1)}, bf16[48,1024]{1,0:T(8,128)(2,1)S(1)}, u32[]{:S(2)}, u32[]{:S(2)}) collective-permute-start(bf16[48,1024]{1,0:T(8,128)(2,1)S(1)} %pad_maximum_fusion.16.refs_0_), channel_id=1, source_target_pairs={{0,18},{2,16},{4,22},{6,20},{8,26},{10,24},{12,30},{14,28},{16,2},... | collective-permute-start | bytes 294920 | tf_op jit(solution)/shard_map/ppermute | solution.py:32
  105.2 6.9 %collective-permute-start.24 = (bf16[48,1152]{1,0:T(8,128)(2,1)}, bf16[48,1152]{1,0:T(8,128)(2,1)S(1)}, u32[]{:S(2)}, u32[]{:S(2)}) collective-permute-start(bf16[48,1152]{1,0:T(8,128)(2,1)} %get-tuple-element.29), channel_id=1, source_target_pairs={{0,18},{2,16},{4,22},{6,20},{8,26},{10,24},{12,30},{14,28},{16,2},... | collective-permute-start | bytes 331784 | tf_op jit(solution)/shard_map/ppermute | solution.py:32
  106.7 5.4 %collective-permute-start.25 = (bf16[48,1152]{1,0:T(8,128)(2,1)}, bf16[48,1152]{1,0:T(8,128)(2,1)S(1)}, u32[]{:S(2)}, u32[]{:S(2)}) collective-permute-start(bf16[48,1152]{1,0:T(8,128)(2,1)} %get-tuple-element.30), channel_id=1, source_target_pairs={{0,16},{2,18},{4,20},{6,22},{8,24},{10,26},{12,28},{14,30},{16,0},... | collective-permute-start | bytes 331784 | tf_op jit(solution)/shard_map/ppermute | solution.py:32
  107.2 6.0 %collective-permute-start.26 = (bf16[48,1152]{1,0:T(8,128)(2,1)}, bf16[48,1152]{1,0:T(8,128)(2,1)S(1)}, u32[]{:S(2)}, u32[]{:S(2)}) collective-permute-start(bf16[48,1152]{1,0:T(8,128)(2,1)} %get-tuple-element.31), channel_id=1, source_target_pairs={{0,2},{2,0},{4,6},{6,4},{8,10},{10,8},{12,14},{14,12},{16,18},{18,... | collective-permute-start | bytes 331784 | tf_op jit(solution)/shard_map/ppermute | solution.py:32
  (21 other events, 223.4 us)
where the time goes:
time: 115 us
  starting transfers between devices  45.4 us (39%)
  waiting for transfers between devices  43.9 us (38%)
  other arithmetic  7.85 us (7%)
  local copies, waits for them, and re-layouts  7.16 us (6%)
  matrix products  4.48 us (4%)
  Pallas kernels  3.6 us (3%)
  blocking collectives  2.09 us (2%)
    ppermute x14, starting transfers between devices, swap_tp(): return lax.ppermute(block, 'tp', route)  32.1 us
    ppermute x1, waiting for transfers between devices, local(): out_came = lax.ppermute(out_sent, ('tp', 'sp'), route)  20.8 us
    ppermute x14, waiting for transfers between devices, swap_tp(): return lax.ppermute(block, 'tp', route)  11.8 us
    ppermute x6, waiting for transfers between devices, swap_in_slab(): return lax.ppermute(block, ('groups', 'tp'), route)  11.3 us
    ppermute x6, starting transfers between devices, swap_in_slab(): return lax.ppermute(block, ('groups', 'tp'), route)  8.06 us
    ppermute x1, starting transfers between devices, local(): out_came = lax.ppermute(out_sent, ('tp', 'sp'), route)  4.14 us
    unnamed x38, local copies, waits for them, and re-layouts  3.68 us
    pallas_call x1, Pallas kernels, project(): pl.pallas_call(lambda *refs: project_kernel(peers, *refs), in_specs=[whol...  3.6 us
  transfers between devices with their start and end apart: 27, of which 9 were waited for; matrix products, arithmetic and copies ran while one was open for 12% of the time, Pallas kernels for 0%

commit v1 on v0

v1 whole, which is shorter than its diff:
```python
import jax
import jax.numpy as jnp
from jax import lax
from jax.experimental import pallas as pl
from jax.experimental.pallas import tpu as pltpu
from jax.sharding import PartitionSpec as P

PRE_SCALE = 144

masked_low = -1e30


def swap_tp(block, flip, only=None):
    count = lax.axis_size("tp")
    route = [(t, t ^ flip) for t in range(count) if only is None or only(t)]
    return lax.ppermute(block, "tp", route)


def swap_sp(block):
    count = lax.axis_size("sp")
    return lax.ppermute(block, "sp", [(s, s ^ 1) for s in range(count)])


def swap_in_slab(block, group_flip, tp_flip):
    groups = lax.axis_size("groups")
    count = lax.axis_size("tp")
    route = [
        (g * count + t, (g ^ group_flip) * count + (t ^ tp_flip))
        for g in range(groups)
        for t in range(count)
    ]
    return lax.ppermute(block, ("groups", "tp"), route)


def fence(*values):
    return lax.optimization_barrier(values)


def angles_of(places, head_dim):
    half_width = head_dim // 2
    spread = jnp.power(
        10000.0, -(jnp.arange(half_width, dtype=jnp.float32) * (2.0 / head_dim))
    )
    angles = places.astype(jnp.float32)[:, None] * spread[None, :]
    return jnp.cos(angles), jnp.sin(angles)


def doc_index(places, doc_ends):
    return jnp.sum((places[:, None] >= doc_ends[None, :]).astype(jnp.int32), axis=1)


def gather_first(block, slabs):
    if slabs != 4:
        return [swap_tp(block, 2 * k) for k in range(1, slabs)]
    return [swap_tp(block, 2), swap_tp(block, 4)]


def gather_last(block, came):
    inner = lambda t: (t >> 1) in (1, 2)
    relayed = swap_tp(came[1], 2, inner)
    return [swap_tp(block, 6, inner), relayed]


def call(kernel, shapes, flags, operands, scratch=()):
    size = sum(x.size * x.dtype.itemsize for x in operands)
    params = None
    if size < 16 << 20:
        operands = [pltpu.with_memory_space_constraint(x, pltpu.VMEM) for x in operands]
        params = pltpu.CompilerParams(vmem_limit_bytes=16 << 20)
    whole = pl.BlockSpec(memory_space=pltpu.VMEM)
    return pl.pallas_call(
        kernel,
        in_specs=[pl.BlockSpec(memory_space=pltpu.SMEM)] + [whole] * len(operands),
        out_specs=[whole] * len(shapes),
        out_shape=[jax.ShapeDtypeStruct(*shape) for shape in shapes],
        scratch_shapes=list(scratch),
        compiler_params=params,
    )(flags, *operands)


def plain(a, w):
    return jnp.dot(a, w, preferred_element_type=jnp.float32)


def turned(a, w):
    return lax.dot_general(a, w, (((1,), (1,)), ((), ())), preferred_element_type=jnp.float32)


def rows_at(blocks, offset, size):
    parts = [block[:, pl.ds(pl.multiple_of(offset, 128), size)] for block in blocks]
    return jnp.concatenate(parts, axis=0) if len(parts) > 1 else parts[0]


def pair_query(blocks, quarters, sp, group):
    size = quarters[0].shape[0]
    total = None
    for i, weight in enumerate(quarters):
        at = (sp ^ (i >> 1)) * 2 + (group ^ (i & 1))
        term = plain(rows_at(blocks, at * size, size), weight[...])
        total = term if total is None else total + term
    return total


def early_kernel(flags, *refs):
    blocks, (w_query, w_kv), quarters, out = refs[:-7], refs[-7:-5], refs[-5:-1], refs[-1]
    head = w_query.shape[1]
    rows = jnp.concatenate([block[...] for block in blocks], axis=0)
    out[:, :head] = plain(rows, w_query[...])
    out[:, head : 2 * head] = turned(rows, w_kv[...])
    out[:, 2 * head :] = pair_query(blocks, quarters, flags[0], flags[3])


def tail_kernel(flags, *refs):
    early, middle, relayed, w_query, w_kv, w_kv_came, w_kv_other, cosine, sine_part = refs[:9]
    quarters, blocks = refs[9:13], refs[13:-3]
    queries, key_value, last = refs[-3:]
    sp, side, inner, group = flags[0], flags[1], flags[2], flags[3]
    head = w_query.shape[1]
    half_head = head // 2
    last[...] = jnp.where(inner != 0, middle[...], relayed[...])
    depth = w_kv_came.shape[1]
    join = lambda a, b: jnp.concatenate([a, b], axis=0)
    own_query = join(early[:, :head], plain(last[...], w_query[...]))
    own_kv = join(early[:, head : 2 * head], turned(last[...], w_kv[...]))
    pair_q = join(early[:, 2 * head :], pair_query([last], quarters, sp, group))
    every = list(blocks) + [last]
    pair_kv = turned(rows_at(every, sp * depth, depth), w_kv_came[...]) + turned(
        rows_at(every, (1 - sp) * depth, depth), w_kv_other[...]
    )
    spin = lambda v: v * cosine[...] + pltpu.roll(v, half_head, 1) * sine_part[...]
    scale = PRE_SCALE ** (-0.5)
    count = own_query.shape[0]
    queries[:count] = (spin(own_query) * scale).astype(queries.dtype)
    queries[count:] = (spin(pair_q) * scale).astype(queries.dtype)
    lane = lax.broadcasted_iota(jnp.int32, own_kv.shape, 1)
    low = lane < half_head
    even = side == 0
    first = jnp.where(even, own_kv, pair_kv)
    second = jnp.where(even, pair_kv, own_kv)
    key_raw = jnp.where(low, first, pltpu.roll(second, half_head, 1))
    key_raw = key_raw.astype(jnp.bfloat16).astype(jnp.float32)
    key_value[:, :head] = spin(key_raw).astype(key_value.dtype)
    value = jnp.where(low, pltpu.roll(first, half_head, 1), second)
    key_value[:, head:] = value.astype(key_value.dtype)


def project_kernel(peers, flags, *refs):
    stacked, pieces, outs = refs[:peers], refs[peers:-peers], refs[-peers:]
    count, width = outs[0].shape
    rows = jnp.concatenate([m[...] for m in stacked], axis=0)
    step = 384 if width % 384 == 0 else width
    for at in range(0, width, step):
        weight = jnp.concatenate([p[:, at : at + step] for p in pieces], axis=0)
        total = plain(rows, weight)
        for i, out in enumerate(outs):
            out[:, at : at + step] = total[i * count : (i + 1) * count].astype(out.dtype)


def assemble_kernel(flags, *refs):
    pieces, out = refs[:-1], refs[-1]
    width = pieces[0].shape[1]
    for i, piece in enumerate(pieces):
        at = pl.multiple_of((flags[4] ^ i) * width, 128)
        out[:, pl.ds(at, width)] = piece[...]


def local(tokens, w_query, w_key, w_value, w_out, doc_lengths):
    rows, width = tokens.shape
    tp_count = lax.axis_size("tp")
    sp_count = lax.axis_size("sp")
    sp_place = lax.axis_index("sp")
    tp_place = lax.axis_index("tp")
    slabs = tp_count // 2
    slab = tp_place // 2
    side = tp_place % 2
    head_dim = w_query.shape[1]

    group = lax.axis_index("groups") % 2
    depth = width // sp_count
    quarter = w_out.shape[1] // 4
    mine = group * 2 + side
    inner = ((slab == 1) | (slab == 2)).astype(jnp.int32)
    flags = jnp.stack([sp_place, side, inner, group, mine]).astype(jnp.int32)
    wkv_own = jnp.concatenate([w_key.T, w_value.T], axis=0)
    share_q = lax.dynamic_slice_in_dim(
        w_query, (sp_place * 2 + group) * (depth // 2), depth // 2, 0
    )
    share_kv = lax.dynamic_slice_in_dim(wkv_own, sp_place * depth, depth, 1)
    out_sent = lax.dynamic_slice_in_dim(w_out, (mine ^ 1) * quarter, quarter, 1)
    share_q, share_kv, out_sent, tokens, doc_lengths, out_weight = fence(
        share_q, share_kv, out_sent, tokens, doc_lengths, w_out
    )
    came = gather_first(tokens, slabs)
    route = [
        ((t * sp_count + s), ((t ^ 1) * sp_count + s))
        for t in range(tp_count)
        for s in range(sp_count)
        if s == t % 2
    ]
    out_came = lax.ppermute(out_sent, ("tp", "sp"), route)
    came_q = swap_tp(share_q, 1)
    cross_q = swap_in_slab(came_q, 1, 0)
    came_kv = swap_tp(share_kv, 1)
    other_kv = swap_sp(came_kv)
    quarters = [came_q, cross_q, swap_sp(came_q), swap_sp(cross_q)]
    out_kept = lax.dynamic_slice_in_dim(out_weight, mine * quarter, quarter, 1)
    out_head = jnp.where(side == sp_place, out_kept, out_came)
    out_first = gather_first(out_head, slabs)

    if slabs == 4:
        last = gather_last(tokens, came)
        firsts = [tokens] + came
    else:
        last = [came[-1], came[-1]]
        firsts = [tokens] + came[:-1]
    early = call(
        early_kernel,
        [((len(firsts) * rows, 3 * head_dim), jnp.float32)],
        flags,
        [*firsts, w_query, wkv_own, *quarters],
    )[0]

    doc_ends = jnp.cumsum(doc_lengths)
    row_ids = jnp.arange(rows, dtype=jnp.int32)
    slab_ids = slab ^ jnp.arange(slabs, dtype=jnp.int32)

    def places_of(at_side, at_sp):
        starts = ((slab_ids * 2 + at_side) * sp_count + at_sp) * rows
        return (starts[:, None] + row_ids[None, :]).reshape(-1)

    places = places_of(side, sp_place)
    cosine, sine_part = angles_of(places, head_dim)
    cosine = jnp.concatenate([cosine, cosine], axis=1)
    sine_part = jnp.concatenate([-sine_part, sine_part], axis=1)
    total_rows = slabs * rows
    queries, key_value = call(
        tail_kernel,
        [((2 * total_rows, head_dim), jnp.bfloat16), ((total_rows, 2 * head_dim), jnp.bfloat16)],
        flags,
        [early, *last, w_query, wkv_own, came_kv, other_kv, cosine, sine_part]
        + quarters
        + firsts,
        [pltpu.VMEM((rows, width), jnp.bfloat16)],
    )
    both = jnp.concatenate([key_value, swap_tp(key_value, 1)], axis=0)
    every = lax.all_gather(both, "sp", axis=0, tiled=True)
    key_places = jnp.concatenate(
        [places_of(b, s) for s in range(sp_count) for b in (side, 1 - side)]
    )
    key_docs = doc_index(key_places, doc_ends)
    query_docs = doc_index(places, doc_ends)
    allowed = (key_places[None, :] <= places[:, None]) & (key_docs[None, :] == query_docs[:, None])
    allowed = jnp.concatenate([allowed, allowed], axis=0)
    scores = jnp.einsum(
        "qd,kd->qk", queries, every[:, :head_dim], preferred_element_type=jnp.float32
    )
    largest = jnp.max(jnp.where(allowed, scores, masked_low), axis=1, keepdims=True)
    weights = jnp.where(allowed, jnp.exp(scores - largest), 0.0)
    denominator = jnp.sum(weights, axis=1, keepdims=True)
    mixed = jnp.dot(
        weights.astype(jnp.bfloat16), every[:, head_dim:], preferred_element_type=jnp.float32
    )
    mixed = (mixed / denominator).astype(jnp.bfloat16)
    count = slabs * rows
    lower, upper = mixed[:count], mixed[count:]
    straight = side == sp_place
    mixed = jnp.concatenate(
        [jnp.where(straight, lower, upper), jnp.where(straight, upper, lower)], axis=1
    )
    parts = [mixed[:rows]]
    for k in range(1, slabs):
        parts.append(swap_tp(mixed[k * rows : (k + 1) * rows], 2 * k))
    out_last = gather_last(out_head, out_first) if slabs == 4 else []
    merged = jnp.concatenate(parts, axis=1)
    peers = ((0, 0), (1, 0), (0, 1), (1, 1))
    stacked = [merged] + [swap_in_slab(merged, g, t) for g, t in peers[1:]]
    if slabs == 4:
        *out_last, stacked[1] = fence(*out_last, stacked[1])
    out_pieces = []
    picked = [jnp.where(inner != 0, *out_last)] if out_last else []
    for piece in [out_head] + out_first + picked:
        out_pieces += [piece, swap_sp(piece)]
    outs = call(
        lambda *refs: project_kernel(len(peers), *refs),
        [((rows, quarter), jnp.bfloat16)] * len(peers),
        flags,
        stacked + out_pieces,
    )
    outs = [outs[0]] + [swap_in_slab(o, g, t) for o, (g, t) in zip(outs[1:], peers[1:])]
    pieces = [outs[0], outs[2], outs[1], outs[3]]
    return call(assemble_kernel, [((rows, width), jnp.bfloat16)], flags, pieces)[0]


def solution(mesh):
    placed = (
        P(("groups", "tp", "sp"), None),
        P(None, "tp"),
        P(None, "tp"),
        P(None, "tp"),
        P("tp", None),
        P("groups"),
    )

    return jax.shard_map(
        local,
        mesh=mesh,
        in_specs=placed,
        out_specs=P(("groups", "tp", "sp"), None),
        check_vma=False,
    )
```

time: 115 us -> 104 us (0.904)
  waiting for transfers between devices: 43.9 us -> 29.2 us
  Pallas kernels: 3.6 us -> 8.72 us
  matrix products: 4.48 us -> 0.83 us
  other arithmetic: 7.85 us -> 11.1 us
  local copies, waits for them, and re-layouts: 7.16 us -> 5.84 us
    ppermute x1, waiting for transfers between devices: 20.8 us -> 0.01 us  [local(): out_came = lax.ppermute(out_sent, ('tp', 'sp'), route)]
    ppermute x14, waiting for transfers between devices: 11.8 us -> 17.2 us  [swap_tp(): return lax.ppermute(block, 'tp', route)]
    pallas_call x1 -> x4, Pallas kernels: 3.6 us -> 8.72 us  [call(): pl.pallas_call(kernel, in_specs=[pl.BlockSpec(memory_space=pltpu.SMEM)] +...]
    unnamed x38 -> x12, local copies, waits for them, and re-layouts: 3.68 us -> 0.03 us
    dot_general x8 -> x0, matrix products: 3.6 us -> none  [the longest x4 1.95 us: local(): jnp.einsum('rk,ck->rc', a, w, preferred_element_type=jnp.float32)]
    add x5, local copies, waits for them, and re-layouts: 0.42 us -> 2.89 us  [places_of(): return (starts[:, None] + row_ids[None, :]).reshape(-1)]
    select_n x5 -> x1, other arithmetic: 2.28 us -> 0.04 us  [local(): picked = [jnp.where(inner != 0, *out_last)] if out_last else []]
    ppermute x6 -> x7, starting transfers between devices: 8.06 us -> 9.63 us  [swap_in_slab(): return lax.ppermute(block, ('groups', 'tp'), route)]
  transfers between devices with their start and end apart: 27 -> 29, of which waited for: 9 -> 9; matrix products, arithmetic and copies ran while one was open for 12% -> 13% of each run, Pallas kernels for 0% -> 5%
where the time goes in v1:
time: 104 us
  starting transfers between devices  46 us (44%)
  waiting for transfers between devices  29.2 us (28%)
  other arithmetic  11.1 us (11%)
  Pallas kernels  8.72 us (8%)
  local copies, waits for them, and re-layouts  5.84 us (6%)
  blocking collectives  2.09 us (2%)
    ppermute x14, starting transfers between devices, swap_tp(): return lax.ppermute(block, 'tp', route)  30.9 us
    ppermute x14, waiting for transfers between devices, swap_tp(): return lax.ppermute(block, 'tp', route)  17.2 us
    ppermute x7, waiting for transfers between devices, swap_in_slab(): return lax.ppermute(block, ('groups', 'tp'), route)  11.9 us
    ppermute x7, starting transfers between devices, swap_in_slab(): return lax.ppermute(block, ('groups', 'tp'), route)  9.63 us
    pallas_call x4, Pallas kernels, call(): pl.pallas_call(kernel, in_specs=[pl.BlockSpec(memory_space=pltpu.SMEM)] +...  8.72 us
    ppermute x1, starting transfers between devices, local(): out_came = lax.ppermute(out_sent, ('tp', 'sp'), route)  4.13 us
    add x5, local copies, waits for them, and re-layouts, places_of(): return (starts[:, None] + row_ids[None, :]).reshape(-1)  2.89 us
    all_gather x1, blocking collectives, local(): every = lax.all_gather(both, 'sp', axis=0, tiled=True)  2.09 us
  transfers between devices with their start and end apart: 29, of which 9 were waited for; matrix products, arithmetic and copies ran while one was open for 13% of the time, Pallas kernels for 5%

profile of v1, /device:TPU:0, one launch (start us, length us, event | category | flops | bytes accessed | tf_op | source)
XLA Modules:
  0.0 104.0 jit_solution(10587486731669063421)
XLA Ops:
  1.1 1.8 %constant_dynamic-slice_fusion.1 = bf16[1152,128]{1,0:T(8,128)(2,1)} fusion(bf16[4608,128]{1,0:T(8,128)(2,1)} %refs_3_.3, s32[]{:T(128)S(6)} %select_n.64), kind=kLoop, calls=%fused_computation.47 | loop fusion | bytes 589828 | tf_op jit(solution)/shard_map/dynamic_slice | solution.py:185
  3.7 3.1 %collective-permute-start = (bf16[48,4608]{1,0:T(8,128)(2,1)S(1)}, bf16[48,4608]{1,0:T(8,128)(2,1)S(1)}, u32[]{:S(2)}, u32[]{:S(2)}) collective-permute-start(bf16[48,4608]{1,0:T(8,128)(2,1)S(1)} %copy-done.1), channel_id=1, source_target_pairs={{0,4},{2,6},{4,0},{6,2},{8,12},{10,14},{12,8},{14,10},{1,5},{3,7},... | collective-permute-start | bytes 1327112 | tf_op jit(solution)/shard_map/ppermute | solution.py:16
  6.8 2.6 %collective-permute-start.1 = (bf16[48,4608]{1,0:T(8,128)(2,1)S(1)}, bf16[48,4608]{1,0:T(8,128)(2,1)}, u32[]{:S(2)}, u32[]{:S(2)}) collective-permute-start(bf16[48,4608]{1,0:T(8,128)(2,1)S(1)} %copy-done.1), channel_id=1, source_target_pairs={{0,8},{2,10},{4,12},{6,14},{8,0},{10,2},{12,4},{14,6},{1,9},{3,11}... | collective-permute-start | bytes 1327112 | tf_op jit(solution)/shard_map/ppermute | solution.py:16
  9.4 1.5 %collective-permute-start.2 = (bf16[1152,128]{1,0:T(8,128)(2,1)}, bf16[1152,128]{1,0:T(8,128)(2,1)}, u32[]{:S(2)}, u32[]{:S(2)}) collective-permute-start(bf16[1152,128]{1,0:T(8,128)(2,1)} %constant_dynamic-slice_fusion.1), channel_id=1, source_target_pairs={{0,2},{2,0},{4,6},{6,4},{8,10},{10,8},{12,14},{14,12},{1,3},{3,1},... | collective-permute-start | bytes 884744 | tf_op jit(solution)/shard_map/ppermute | solution.py:16
  11.4 4.1 %collective-permute-start.14 = (bf16[128,1152]{1,0:T(8,128)(2,1)S(1)}, bf16[128,1152]{1,0:T(8,128)(2,1)}, u32[]{:S(2)}, u32[]{:S(2)}) collective-permute-start(bf16[128,1152]{1,0:T(8,128)(2,1)S(1)} %constant_dynamic-slice_fusion), channel_id=1, source_target_pairs={{0,2},{3,1},{4,6},{7,5},{8,10},{11,9},{12,14},{15,13},{16,18},{19,... | collective-permute-start | bytes 884744 | tf_op jit(solution)/shard_map/ppermute | solution.py:200
  26.9 5.3 %collective-permute-done.8.refs_5_ = bf16[128,2304]{1,0:T(8,128)(2,1)} collective-permute-done((bf16[128,2304]{1,0:T(8,128)(2,1)}, bf16[128,2304]{1,0:T(8,128)(2,1)}, u32[]{:S(2)}, u32[]{:S(2)}) %collective-permute-start.8) | collective-permute-done | bytes 589856 | tf_op jit(solution)/shard_map/ppermute | solution.py:16
  36.8 3.2 %collective-permute-start.16 = (bf16[128,1152]{1,0:T(8,128)(2,1)S(1)}, bf16[128,1152]{1,0:T(8,128)(2,1)}, u32[]{:S(2)}, u32[]{:S(2)}) collective-permute-start(bf16[128,1152]{1,0:T(8,128)(2,1)S(1)} %dynamic-slice_select_fusion.refs_5_), channel_id=1, source_target_pairs={{0,8},{2,10},{4,12},{6,14},{8,0},{10,2},{12,4},{14,6},{1,9},{3,11}... | collective-permute-start | bytes 884744 | tf_op jit(solution)/shard_map/ppermute | solution.py:16
  40.8 2.5 %shard_map.64.refs_0_ = f32[144,384]{1,0:T(8,128)S(1)} custom-call(s32[5]{0:T(128)S(1)} %stack.23.flags.refs_0_, bf16[48,4608]{1,0:T(8,128)(2,1)S(1)} %copy-done.1, bf16[48,4608]{1,0:T(8,128)(2,1)S(1)} %collective-permute-done.refs_1_.refs_14_, bf16[48,4608]{1,0:T(8,128)(2,1)} %collective-permute-done.1.refs_2_.refs_15_, bf16[4608,128]{1,0:T(8,128)(2,1)S(1)} %copy-done, ...), custom_call_target="tpu_custom_call" | custom-call | tf_op jit(solution)/shard_map/pallas_call | solution.py:71
  43.4 5.2 %collective-permute-done.7.refs_2_ = bf16[48,4608]{1,0:T(8,128)(2,1)S(1)} collective-permute-done((bf16[48,4608]{1,0:T(8,128)(2,1)}, bf16[48,4608]{1,0:T(8,128)(2,1)S(1)}, u32[]{:S(2)}, u32[]{:S(2)}) %collective-permute-start.7) | collective-permute-done | bytes 442400 | tf_op jit(solution)/shard_map/ppermute | solution.py:16
  48.6 3.1 %shard_map.65 = (bf16[384,128]{1,0:T(8,128)(2,1)S(1)}, bf16[192,256]{1,0:T(8,128)(2,1)S(1)}) custom-call(s32[5]{0:T(128)S(1)} %stack.23.flags.refs_0_, f32[144,384]{1,0:T(8,128)S(1)} %shard_map.64.refs_0_, bf16[48,4608]{1,0:T(8,128)(2,1)S(1)} %collective-permute-done.6.refs_1_, bf16[48,4608]{1,0:T(8,128)(2,1)S(1)} %collective-permute-done.7.refs_2_, ...), custom_call_target="tpu_custom_call" | custom-call | tf_op jit(solution)/shard_map/pallas_call | solution.py:71
  51.7 2.2 %collective-permute-start.10 = (bf16[192,256]{1,0:T(8,128)(2,1)S(1)}, bf16[192,256]{1,0:T(8,128)(2,1)S(1)}, u32[]{:S(2)}, u32[]{:S(2)}) collective-permute-start(bf16[192,256]{1,0:T(8,128)(2,1)S(1)} %get-tuple-element.25), channel_id=1, source_target_pairs={{0,2},{2,0},{4,6},{6,4},{8,10},{10,8},{12,14},{14,12},{1,3},{3,1},... | collective-permute-start | bytes 294920 | tf_op jit(solution)/shard_map/ppermute | solution.py:16
  54.8 7.9 %collective-permute-start.22 = (bf16[128,1152]{1,0:T(8,128)(2,1)S(1)}, bf16[128,1152]{1,0:T(8,128)(2,1)S(1)}, u32[]{:S(2)}, u32[]{:S(2)}) collective-permute-start(bf16[128,1152]{1,0:T(8,128)(2,1)S(1)} %dynamic-slice_select_fusion.refs_5_), channel_id=1, source_target_pairs={{0,4},{2,6},{4,0},{6,2},{8,12},{10,14},{12,8},{14,10},{1,5},{3,7},... | collective-permute-start | bytes 884744 | tf_op jit(solution)/shard_map/ppermute | solution.py:16
  64.0 2.1 %all_gather.3 = bf16[768,256]{1,0:T(8,128)(2,1)S(1)} all-gather(bf16[384,256]{1,0:T(8,128)(2,1)S(1)} %pad_maximum_fusion.1), channel_id=1, replica_groups=mesh['groups'=2,'tp'=8,'sp'=2] {'sp'}, dimensions={0}, use_global_device_ids=true | all-gather | bytes 589824 | tf_op jit(solution)/shard_map/all_gather | solution.py:246
  67.4 2.7 %collective-permute-start.11 = (bf16[48,256]{1,0:T(8,128)(2,1)S(1)}, bf16[48,256]{1,0:T(8,128)(2,1)S(1)}, u32[]{:S(2)}, u32[]{:S(2)}) collective-permute-start(bf16[48,256]{1,0:T(8,128)(2,1)S(1)} %get-tuple-element.36), channel_id=1, source_target_pairs={{0,4},{2,6},{4,0},{6,2},{8,12},{10,14},{12,8},{14,10},{1,5},{3,7},... | collective-permute-start | bytes 73736 | tf_op jit(solution)/shard_map/ppermute | solution.py:16
  71.2 3.3 %collective-permute-done.11 = bf16[48,256]{1,0:T(8,128)(2,1)S(1)} collective-permute-done((bf16[48,256]{1,0:T(8,128)(2,1)S(1)}, bf16[48,256]{1,0:T(8,128)(2,1)S(1)}, u32[]{:S(2)}, u32[]{:S(2)}) %collective-permute-start.11) | collective-permute-done | bytes 24608 | tf_op jit(solution)/shard_map/ppermute | solution.py:16
  74.5 2.2 %collective-permute-start.13 = (bf16[48,256]{1,0:T(8,128)(2,1)S(1)}, bf16[48,256]{1,0:T(8,128)(2,1)S(1)}, u32[]{:S(2)}, u32[]{:S(2)}) collective-permute-start(bf16[48,256]{1,0:T(8,128)(2,1)S(1)} %get-tuple-element.37), channel_id=1, source_target_pairs={{0,12},{2,14},{4,8},{6,10},{8,4},{10,6},{12,0},{14,2},{1,13},{3,15... | collective-permute-start | bytes 73736 | tf_op jit(solution)/shard_map/ppermute | solution.py:16
  76.7 3.5 %collective-permute-done.13 = bf16[48,256]{1,0:T(8,128)(2,1)S(1)} collective-permute-done((bf16[48,256]{1,0:T(8,128)(2,1)S(1)}, bf16[48,256]{1,0:T(8,128)(2,1)S(1)}, u32[]{:S(2)}, u32[]{:S(2)}) %collective-permute-start.13) | collective-permute-done | bytes 24608 | tf_op jit(solution)/shard_map/ppermute | solution.py:16
  80.2 1.6 %collective-permute-start.18 = (bf16[48,1024]{1,0:T(8,128)(2,1)S(1)}, bf16[48,1024]{1,0:T(8,128)(2,1)S(1)}, u32[]{:S(2)}, u32[]{:S(2)}) collective-permute-start(bf16[48,1024]{1,0:T(8,128)(2,1)S(1)} %pad_maximum_fusion.4.refs_1_), channel_id=1, source_target_pairs={{0,16},{2,18},{4,20},{6,22},{8,24},{10,26},{12,28},{14,30},{16,0},... | collective-permute-start | bytes 294920 | tf_op jit(solution)/shard_map/ppermute | solution.py:32
  82.3 2.5 %collective-permute-done.18.refs_2_ = bf16[48,1024]{1,0:T(8,128)(2,1)S(1)} collective-permute-done((bf16[48,1024]{1,0:T(8,128)(2,1)S(1)}, bf16[48,1024]{1,0:T(8,128)(2,1)S(1)}, u32[]{:S(2)}, u32[]{:S(2)}) %collective-permute-start.18) | collective-permute-done | bytes 98336 | tf_op jit(solution)/shard_map/ppermute | solution.py:32
  86.3 1.7 %collective-permute-start.20 = (bf16[48,1024]{1,0:T(8,128)(2,1)S(1)}, bf16[48,1024]{1,0:T(8,128)(2,1)S(1)}, u32[]{:S(2)}, u32[]{:S(2)}) collective-permute-start(bf16[48,1024]{1,0:T(8,128)(2,1)S(1)} %pad_maximum_fusion.4.refs_1_), channel_id=1, source_target_pairs={{0,18},{2,16},{4,22},{6,20},{8,26},{10,24},{12,30},{14,28},{16,2},... | collective-permute-start | bytes 294920 | tf_op jit(solution)/shard_map/ppermute | solution.py:32
  88.0 4.3 %collective-permute-done.19.refs_3_ = bf16[48,1024]{1,0:T(8,128)(2,1)S(1)} collective-permute-done((bf16[48,1024]{1,0:T(8,128)(2,1)S(1)}, bf16[48,1024]{1,0:T(8,128)(2,1)S(1)}, u32[]{:S(2)}, u32[]{:S(2)}) %collective-permute-start.19) | collective-permute-done | bytes 98336 | tf_op jit(solution)/shard_map/ppermute | solution.py:32
  92.3 1.8 %shard_map.66 = (bf16[48,1152]{1,0:T(8,128)(2,1)S(1)}, bf16[48,1152]{1,0:T(8,128)(2,1)S(1)}, bf16[48,1152]{1,0:T(8,128)(2,1)S(1)}, bf16[48,1152]{1,0:T(8,128)(2,1)S(1)}) custom-call(s32[5]{0:T(128)S(1)} %stack.23.flags.refs_0_, bf16[48,1024]{1,0:T(8,128)(2,1)S(1)} %pad_maximum_fusion.4.refs_1_, bf16[48,1024]{1,0:T(8,128)(2,1)S(1)} %collective-permute-done.18.refs_2_, ...), custom_call_target="tpu_custom_call" | custom-call | tf_op jit(solution)/shard_map/pallas_call | solution.py:71
  98.8 2.0 %collective-permute-done.27.refs_2_ = bf16[48,1152]{1,0:T(8,128)(2,1)S(1)} collective-permute-done((bf16[48,1152]{1,0:T(8,128)(2,1)S(1)}, bf16[48,1152]{1,0:T(8,128)(2,1)S(1)}, u32[]{:S(2)}, u32[]{:S(2)}) %collective-permute-start.27) | collective-permute-done | bytes 110624 | tf_op jit(solution)/shard_map/ppermute | solution.py:32
  100.8 1.9 %collective-permute-done.28.refs_3_ = bf16[48,1152]{1,0:T(8,128)(2,1)S(1)} collective-permute-done((bf16[48,1152]{1,0:T(8,128)(2,1)S(1)}, bf16[48,1152]{1,0:T(8,128)(2,1)S(1)}, u32[]{:S(2)}, u32[]{:S(2)}) %collective-permute-start.28) | collective-permute-done | bytes 110624 | tf_op jit(solution)/shard_map/ppermute | solution.py:32
  (88 shorter events, 31.9 us)
Async XLA Ops:
  3.7 30.1 %collective-permute-start = (bf16[48,4608]{1,0:T(8,128)(2,1)S(1)}, bf16[48,4608]{1,0:T(8,128)(2,1)S(1)}, u32[]{:S(2)}, u32[]{:S(2)}) collective-permute-start(bf16[48,4608]{1,0:T(8,128)(2,1)S(1)} %copy-done.1), channel_id=1, source_target_pairs={{0,4},{2,6},{4,0},{6,2},{8,12},{10,14},{12,8},{14,10},{1,5},{3,7},... | collective-permute-start | bytes 1327112 | tf_op jit(solution)/shard_map/ppermute | solution.py:16
  6.8 27.6 %collective-permute-start.1 = (bf16[48,4608]{1,0:T(8,128)(2,1)S(1)}, bf16[48,4608]{1,0:T(8,128)(2,1)}, u32[]{:S(2)}, u32[]{:S(2)}) collective-permute-start(bf16[48,4608]{1,0:T(8,128)(2,1)S(1)} %copy-done.1), channel_id=1, source_target_pairs={{0,8},{2,10},{4,12},{6,14},{8,0},{10,2},{12,4},{14,6},{1,9},{3,11}... | collective-permute-start | bytes 1327112 | tf_op jit(solution)/shard_map/ppermute | solution.py:16
  9.4 14.6 %collective-permute-start.2 = (bf16[1152,128]{1,0:T(8,128)(2,1)}, bf16[1152,128]{1,0:T(8,128)(2,1)}, u32[]{:S(2)}, u32[]{:S(2)}) collective-permute-start(bf16[1152,128]{1,0:T(8,128)(2,1)} %constant_dynamic-slice_fusion.1), channel_id=1, source_target_pairs={{0,2},{2,0},{4,6},{6,4},{8,10},{10,8},{12,14},{14,12},{1,3},{3,1},... | collective-permute-start | bytes 884744 | tf_op jit(solution)/shard_map/ppermute | solution.py:16
  10.9 21.3 %collective-permute-start.8 = (bf16[128,2304]{1,0:T(8,128)(2,1)}, bf16[128,2304]{1,0:T(8,128)(2,1)}, u32[]{:S(2)}, u32[]{:S(2)}) collective-permute-start(bf16[128,2304]{1,0:T(8,128)(2,1)} %fusion.4), channel_id=1, source_target_pairs={{0,2},{2,0},{4,6},{6,4},{8,10},{10,8},{12,14},{14,12},{1,3},{3,1},... | collective-permute-start | bytes 1769480 | tf_op jit(solution)/shard_map/ppermute | solution.py:16
  11.4 21.7 %collective-permute-start.14 = (bf16[128,1152]{1,0:T(8,128)(2,1)S(1)}, bf16[128,1152]{1,0:T(8,128)(2,1)}, u32[]{:S(2)}, u32[]{:S(2)}) collective-permute-start(bf16[128,1152]{1,0:T(8,128)(2,1)S(1)} %constant_dynamic-slice_fusion), channel_id=1, source_target_pairs={{0,2},{3,1},{4,6},{7,5},{8,10},{11,9},{12,14},{15,13},{16,18},{19,... | collective-permute-start | bytes 884744 | tf_op jit(solution)/shard_map/ppermute | solution.py:200
  24.0 11.7 %collective-permute-start.3 = (bf16[1152,128]{1,0:T(8,128)(2,1)}, bf16[1152,128]{1,0:T(8,128)(2,1)}, u32[]{:S(2)}, u32[]{:S(2)}) collective-permute-start(bf16[1152,128]{1,0:T(8,128)(2,1)} %collective-permute-done.2.refs_5_.refs_9_), channel_id=1, source_target_pairs={{0,16},{2,18},{4,20},{6,22},{8,24},{10,26},{12,28},{14,30},{16,0},... | collective-permute-start | bytes 884744 | tf_op jit(solution)/shard_map/ppermute | solution.py:32
  32.2 16.4 %collective-permute-start.9 = (bf16[128,2304]{1,0:T(8,128)(2,1)}, bf16[128,2304]{1,0:T(8,128)(2,1)}, u32[]{:S(2)}, u32[]{:S(2)}) collective-permute-start(bf16[128,2304]{1,0:T(8,128)(2,1)} %collective-permute-done.8.refs_5_), channel_id=1, source_target_pairs={{0,1},{1,0},{2,3},{3,2},{4,5},{5,4},{6,7},{7,6},{8,9},{9,8},{10,11... | collective-permute-start | bytes 1769480 | tf_op jit(solution)/shard_map/ppermute | solution.py:21
  33.1 10.3 %collective-permute-start.6 = (bf16[48,4608]{1,0:T(8,128)(2,1)S(1)}, bf16[48,4608]{1,0:T(8,128)(2,1)S(1)}, u32[]{:S(2)}, u32[]{:S(2)}) collective-permute-start(bf16[48,4608]{1,0:T(8,128)(2,1)S(1)} %copy-done.1), channel_id=1, source_target_pairs={{4,8},{6,10},{8,4},{10,6},{5,9},{7,11},{9,5},{11,7},{20,24},{22,26... | collective-permute-start | bytes 1327112 | tf_op jit(solution)/shard_map/ppermute | solution.py:16
  34.4 14.2 %collective-permute-start.7 = (bf16[48,4608]{1,0:T(8,128)(2,1)}, bf16[48,4608]{1,0:T(8,128)(2,1)S(1)}, u32[]{:S(2)}, u32[]{:S(2)}) collective-permute-start(bf16[48,4608]{1,0:T(8,128)(2,1)} %collective-permute-done.1.refs_2_.refs_15_), channel_id=1, source_target_pairs={{4,0},{6,2},{8,12},{10,14},{5,1},{7,3},{9,13},{11,15},{20,16},{22,... | collective-permute-start | bytes 1327112 | tf_op jit(solution)/shard_map/ppermute | solution.py:16
  36.8 25.9 %collective-permute-start.16 = (bf16[128,1152]{1,0:T(8,128)(2,1)S(1)}, bf16[128,1152]{1,0:T(8,128)(2,1)}, u32[]{:S(2)}, u32[]{:S(2)}) collective-permute-start(bf16[128,1152]{1,0:T(8,128)(2,1)S(1)} %dynamic-slice_select_fusion.refs_5_), channel_id=1, source_target_pairs={{0,8},{2,10},{4,12},{6,14},{8,0},{10,2},{12,4},{14,6},{1,9},{3,11}... | collective-permute-start | bytes 884744 | tf_op jit(solution)/shard_map/ppermute | solution.py:16
  51.7 12.3 %collective-permute-start.10 = (bf16[192,256]{1,0:T(8,128)(2,1)S(1)}, bf16[192,256]{1,0:T(8,128)(2,1)S(1)}, u32[]{:S(2)}, u32[]{:S(2)}) collective-permute-start(bf16[192,256]{1,0:T(8,128)(2,1)S(1)} %get-tuple-element.25), channel_id=1, source_target_pairs={{0,2},{2,0},{4,6},{6,4},{8,10},{10,8},{12,14},{14,12},{1,3},{3,1},... | collective-permute-start | bytes 294920 | tf_op jit(solution)/shard_map/ppermute | solution.py:16
  54.1 27.6 %collective-permute-start.15 = (bf16[128,1152]{1,0:T(8,128)(2,1)S(1)}, bf16[128,1152]{1,0:T(8,128)(2,1)S(1)}, u32[]{:S(2)}, u32[]{:S(2)}) collective-permute-start(bf16[128,1152]{1,0:T(8,128)(2,1)S(1)} %dynamic-slice_select_fusion.refs_5_), channel_id=1, source_target_pairs={{4,8},{6,10},{8,4},{10,6},{5,9},{7,11},{9,5},{11,7},{20,24},{22,26... | collective-permute-start | bytes 884744 | tf_op jit(solution)/shard_map/ppermute | solution.py:16
  54.8 27.5 %collective-permute-start.22 = (bf16[128,1152]{1,0:T(8,128)(2,1)S(1)}, bf16[128,1152]{1,0:T(8,128)(2,1)S(1)}, u32[]{:S(2)}, u32[]{:S(2)}) collective-permute-start(bf16[128,1152]{1,0:T(8,128)(2,1)S(1)} %dynamic-slice_select_fusion.refs_5_), channel_id=1, source_target_pairs={{0,4},{2,6},{4,0},{6,2},{8,12},{10,14},{12,8},{14,10},{1,5},{3,7},... | collective-permute-start | bytes 884744 | tf_op jit(solution)/shard_map/ppermute | solution.py:16
  62.7 19.6 %collective-permute-start.17 = (bf16[128,1152]{1,0:T(8,128)(2,1)}, bf16[128,1152]{1,0:T(8,128)(2,1)S(1)}, u32[]{:S(2)}, u32[]{:S(2)}) collective-permute-start(bf16[128,1152]{1,0:T(8,128)(2,1)} %collective-permute-done.16.refs_9_), channel_id=1, source_target_pairs={{4,0},{6,2},{8,12},{10,14},{5,1},{7,3},{9,13},{11,15},{20,16},{22,... | collective-permute-start | bytes 884744 | tf_op jit(solution)/shard_map/ppermute | solution.py:16
  67.4 7.1 %collective-permute-start.11 = (bf16[48,256]{1,0:T(8,128)(2,1)S(1)}, bf16[48,256]{1,0:T(8,128)(2,1)S(1)}, u32[]{:S(2)}, u32[]{:S(2)}) collective-permute-start(bf16[48,256]{1,0:T(8,128)(2,1)S(1)} %get-tuple-element.36), channel_id=1, source_target_pairs={{0,4},{2,6},{4,0},{6,2},{8,12},{10,14},{12,8},{14,10},{1,5},{3,7},... | collective-permute-start | bytes 73736 | tf_op jit(solution)/shard_map/ppermute | solution.py:16
  70.1 6.5 %collective-permute-start.12 = (bf16[48,256]{1,0:T(8,128)(2,1)S(1)}, bf16[48,256]{1,0:T(8,128)(2,1)S(1)}, u32[]{:S(2)}, u32[]{:S(2)}) collective-permute-start(bf16[48,256]{1,0:T(8,128)(2,1)S(1)} %get-tuple-element.38), channel_id=1, source_target_pairs={{0,8},{2,10},{4,12},{6,14},{8,0},{10,2},{12,4},{14,6},{1,9},{3,11}... | collective-permute-start | bytes 73736 | tf_op jit(solution)/shard_map/ppermute | solution.py:16
  74.5 5.6 %collective-permute-start.13 = (bf16[48,256]{1,0:T(8,128)(2,1)S(1)}, bf16[48,256]{1,0:T(8,128)(2,1)S(1)}, u32[]{:S(2)}, u32[]{:S(2)}) collective-permute-start(bf16[48,256]{1,0:T(8,128)(2,1)S(1)} %get-tuple-element.37), channel_id=1, source_target_pairs={{0,12},{2,14},{4,8},{6,10},{8,4},{10,6},{12,0},{14,2},{1,13},{3,15... | collective-permute-start | bytes 73736 | tf_op jit(solution)/shard_map/ppermute | solution.py:16
  81.7 6.3 %collective-permute-start.24 = (bf16[128,1152]{1,0:T(8,128)(2,1)}, bf16[128,1152]{1,0:T(8,128)(2,1)S(1)}, u32[]{:S(2)}, u32[]{:S(2)}) collective-permute-start(bf16[128,1152]{1,0:T(8,128)(2,1)} %collective-permute-done.16.refs_9_), channel_id=1, source_target_pairs={{0,1},{1,0},{2,3},{3,2},{4,5},{5,4},{6,7},{7,6},{8,9},{9,8},{10,11... | collective-permute-start | bytes 884744 | tf_op jit(solution)/shard_map/ppermute | solution.py:21
  82.2 5.8 %collective-permute-start.23 = (bf16[128,1152]{1,0:T(8,128)(2,1)S(1)}, bf16[128,1152]{1,0:T(8,128)(2,1)S(1)}, u32[]{:S(2)}, u32[]{:S(2)}) collective-permute-start(bf16[128,1152]{1,0:T(8,128)(2,1)S(1)} %collective-permute-done.22.refs_7_), channel_id=1, source_target_pairs={{0,1},{1,0},{2,3},{3,2},{4,5},{5,4},{6,7},{7,6},{8,9},{9,8},{10,11... | collective-permute-start | bytes 884744 | tf_op jit(solution)/shard_map/ppermute | solution.py:21
  84.9 7.4 %collective-permute-start.25 = (bf16[128,1152]{1,0:T(8,128)(2,1)S(1)}, bf16[128,1152]{1,0:T(8,128)(2,1)S(1)}, u32[]{:S(2)}, u32[]{:S(2)}) collective-permute-start(bf16[128,1152]{1,0:T(8,128)(2,1)S(1)} %broadcast_select_fusion.refs_11_), channel_id=1, source_target_pairs={{0,1},{1,0},{2,3},{3,2},{4,5},{5,4},{6,7},{7,6},{8,9},{9,8},{10,11... | collective-permute-start | bytes 884744 | tf_op jit(solution)/shard_map/ppermute | solution.py:21
  85.0 7.3 %collective-permute-start.19 = (bf16[48,1024]{1,0:T(8,128)(2,1)S(1)}, bf16[48,1024]{1,0:T(8,128)(2,1)S(1)}, u32[]{:S(2)}, u32[]{:S(2)}) collective-permute-start(bf16[48,1024]{1,0:T(8,128)(2,1)S(1)} %pad_maximum_fusion.4.refs_1_), channel_id=1, source_target_pairs={{0,2},{2,0},{4,6},{6,4},{8,10},{10,8},{12,14},{14,12},{16,18},{18,... | collective-permute-start | bytes 294920 | tf_op jit(solution)/shard_map/ppermute | solution.py:32
  86.3 6.0 %collective-permute-start.20 = (bf16[48,1024]{1,0:T(8,128)(2,1)S(1)}, bf16[48,1024]{1,0:T(8,128)(2,1)S(1)}, u32[]{:S(2)}, u32[]{:S(2)}) collective-permute-start(bf16[48,1024]{1,0:T(8,128)(2,1)S(1)} %pad_maximum_fusion.4.refs_1_), channel_id=1, source_target_pairs={{0,18},{2,16},{4,22},{6,20},{8,26},{10,24},{12,30},{14,28},{16,2},... | collective-permute-start | bytes 294920 | tf_op jit(solution)/shard_map/ppermute | solution.py:32
  95.4 5.4 %collective-permute-start.27 = (bf16[48,1152]{1,0:T(8,128)(2,1)S(1)}, bf16[48,1152]{1,0:T(8,128)(2,1)S(1)}, u32[]{:S(2)}, u32[]{:S(2)}) collective-permute-start(bf16[48,1152]{1,0:T(8,128)(2,1)S(1)} %get-tuple-element.33), channel_id=1, source_target_pairs={{0,16},{2,18},{4,20},{6,22},{8,24},{10,26},{12,28},{14,30},{16,0},... | collective-permute-start | bytes 331784 | tf_op jit(solution)/shard_map/ppermute | solution.py:32
  96.9 5.8 %collective-permute-start.28 = (bf16[48,1152]{1,0:T(8,128)(2,1)S(1)}, bf16[48,1152]{1,0:T(8,128)(2,1)S(1)}, u32[]{:S(2)}, u32[]{:S(2)}) collective-permute-start(bf16[48,1152]{1,0:T(8,128)(2,1)S(1)} %get-tuple-element.34), channel_id=1, source_target_pairs={{0,18},{2,16},{4,22},{6,20},{8,26},{10,24},{12,30},{14,28},{16,2},... | collective-permute-start | bytes 331784 | tf_op jit(solution)/shard_map/ppermute | solution.py:32
  (11 other events, 71.4 us)

commit v2 on v1

v2 whole, which is shorter than its diff:
```python
import jax
import jax.numpy as jnp
from jax import lax
from jax.experimental import pallas as pl
from jax.experimental.pallas import tpu as pltpu
from jax.sharding import PartitionSpec as P

PRE_SCALE = 144

masked_low = -1e30


def swap_tp(block, flip, only=None):
    count = lax.axis_size("tp")
    route = [(t, t ^ flip) for t in range(count) if only is None or only(t)]
    return lax.ppermute(block, "tp", route)


def swap_sp(block):
    count = lax.axis_size("sp")
    return lax.ppermute(block, "sp", [(s, s ^ 1) for s in range(count)])


def swap_by_core(block, flips, only=lambda t: True):
    count, cores = lax.axis_size("tp"), lax.axis_size("sp")
    route = [
        (t * cores + s, (t ^ flips[s]) * cores + s)
        for t in range(count)
        for s in range(cores)
        if only(t)
    ]
    return lax.ppermute(block, ("tp", "sp"), route)


def swap_in_slab(block, group_flip, tp_flip):
    groups = lax.axis_size("groups")
    count = lax.axis_size("tp")
    route = [
        (g * count + t, (g ^ group_flip) * count + (t ^ tp_flip))
        for g in range(groups)
        for t in range(count)
    ]
    return lax.ppermute(block, ("groups", "tp"), route)


def fence(*values):
    return lax.optimization_barrier(values)


def call(kernel, shapes, flags, operands, scratch=(), outs=pltpu.VMEM):
    size = sum(x.size * x.dtype.itemsize for x in operands)
    params = None
    if size < 16 << 20:
        operands = [pltpu.with_memory_space_constraint(x, pltpu.VMEM) for x in operands]
        params = pltpu.CompilerParams(vmem_limit_bytes=16 << 20)
    whole = pl.BlockSpec(memory_space=pltpu.VMEM)
    return pl.pallas_call(
        kernel,
        in_specs=[pl.BlockSpec(memory_space=pltpu.SMEM)] + [whole] * len(operands),
        out_specs=[pl.BlockSpec(memory_space=outs)] * len(shapes),
        out_shape=[jax.ShapeDtypeStruct(*shape) for shape in shapes],
        scratch_shapes=list(scratch),
        compiler_params=params,
    )(flags, *operands)


def plain(a, w):
    return jnp.dot(a, w, preferred_element_type=jnp.float32)


def turned(a, w):
    return lax.dot_general(a, w, (((1,), (1,)), ((), ())), preferred_element_type=jnp.float32)


def rows_at(blocks, offset, size):
    parts = [block[:, pl.ds(pl.multiple_of(offset, 128), size)] for block in blocks]
    return jnp.concatenate(parts, axis=0) if len(parts) > 1 else parts[0]


def products(blocks, weights, sp, group):
    w_query, w_kv, kv_came, kv_other, *quarters = weights
    rows = jnp.concatenate([block[...] for block in blocks], axis=0)
    own_query = plain(rows, w_query[...])
    own_kv = turned(rows, w_kv[...])
    size = quarters[0].shape[0]
    pair_query = None
    for i, weight in enumerate(quarters):
        at = (sp ^ (i >> 1)) * 2 + (group ^ (i & 1))
        term = plain(rows_at(blocks, at * size, size), weight[...])
        pair_query = term if pair_query is None else pair_query + term
    depth = kv_came.shape[1]
    pair_kv = turned(rows_at(blocks, sp * depth, depth), kv_came[...]) + turned(
        rows_at(blocks, (1 - sp) * depth, depth), kv_other[...]
    )
    return own_query, own_kv, pair_query, pair_kv


def early_kernel(flags, *refs):
    blocks, weights, out = refs[:-9], refs[-9:-1], refs[-1]
    head = weights[0].shape[1]
    for i, part in enumerate(products(blocks, weights, flags[0], flags[3])):
        out[:, i * head : (i + 1) * head] = part


def tail_kernel(flags, early, middle, relayed, cosine, sine_part, *refs):
    weights, (queries, key_value, last) = refs[:8], refs[8:]
    side, inner = flags[1], flags[2]
    head = weights[0].shape[1]
    half_head = head // 2
    last[...] = jnp.where(inner != 0, middle[...], relayed[...])
    late = products([last], weights, flags[0], flags[3])
    join = lambda i: jnp.concatenate([early[:, i * head : (i + 1) * head], late[i]], axis=0)
    own_query, own_kv, pair_query, pair_kv = [join(i) for i in range(4)]
    spin = lambda v: v * cosine[...] + pltpu.roll(v, half_head, 1) * sine_part[...]
    scale = PRE_SCALE ** (-0.5)
    count = own_query.shape[0]
    queries[:count] = (spin(own_query) * scale).astype(queries.dtype)
    queries[count:] = (spin(pair_query) * scale).astype(queries.dtype)
    lane = lax.broadcasted_iota(jnp.int32, own_kv.shape, 1)
    low = lane < half_head
    even = side == 0
    first = jnp.where(even, own_kv, pair_kv)
    second = jnp.where(even, pair_kv, own_kv)
    key_raw = jnp.where(low, first, pltpu.roll(second, half_head, 1))
    key_raw = key_raw.astype(jnp.bfloat16).astype(jnp.float32)
    key_value[:, :head] = spin(key_raw).astype(key_value.dtype)
    value = jnp.where(low, pltpu.roll(first, half_head, 1), second)
    key_value[:, head:] = value.astype(key_value.dtype)


def project_kernel(peers, split, flags, *refs):
    stacked, pieces, outs = refs[:peers], list(refs[peers:-peers]), refs[-peers:]
    count, width = outs[0].shape
    rows = jnp.concatenate([m[...] for m in stacked], axis=0)
    step = 384 if width % 384 == 0 else width
    received = flags[2] != flags[0]
    for at in range(0, width, step):
        parts = [p[:, at : at + step] for p in pieces]
        if split:
            parts[-2:] = [jnp.where(received, parts[-2], parts[-1])]
        total = plain(rows, jnp.concatenate(parts, axis=0))
        for i, out in enumerate(outs):
            out[:, at : at + step] = total[i * count : (i + 1) * count].astype(out.dtype)


def assemble_kernel(flags, *refs):
    pieces, out, sems = refs[:-2], refs[-2], refs[-1]
    width = pieces[0].shape[1]
    copies = []
    for i, piece in enumerate(pieces):
        at = pl.multiple_of((flags[4] ^ i) * width, 128)
        copies.append(pltpu.make_async_copy(piece, out.at[:, pl.ds(at, width)], sems.at[i]))
        copies[-1].start()
    for copy in copies:
        copy.wait()


def local(tokens, w_query, w_key, w_value, w_out, doc_lengths):
    rows, width = tokens.shape
    tp_count = lax.axis_size("tp")
    sp_count = lax.axis_size("sp")
    sp_place = lax.axis_index("sp")
    tp_place = lax.axis_index("tp")
    group = lax.axis_index("groups") % 2
    slabs = tp_count // 2
    slab = tp_place // 2
    side = tp_place % 2
    head_dim = w_query.shape[1]
    short = slabs == 4
    is_inner = lambda t: (t >> 1) in (1, 2)

    if short:
        far = swap_tp(tokens, 4)
        middle = swap_tp(tokens, 6, is_inner)
        near = swap_tp(tokens, 2)
        relayed = swap_tp(far, 2, is_inner)
        firsts, last = [tokens, near, far], [middle, relayed]
    else:
        came = [swap_tp(tokens, 2 * k) for k in range(1, slabs)]
        firsts, last = [tokens] + came[:-1], [came[-1], came[-1]]

    depth = width // sp_count
    quarter = w_out.shape[1] // 4
    mine = group * 2 + side
    inner = ((slab == 1) | (slab == 2)).astype(jnp.int32)
    flags = jnp.stack([sp_place, side, inner, group, mine]).astype(jnp.int32)
    w_kv = jnp.concatenate([w_key.T, w_value.T], axis=0)
    share_q = lax.dynamic_slice_in_dim(
        w_query, (sp_place * 2 + group) * (depth // 2), depth // 2, 0
    )
    share_kv = lax.dynamic_slice_in_dim(w_kv, sp_place * depth, depth, 1)
    share_q, share_kv, doc_lengths, w_out = fence(share_q, share_kv, doc_lengths, w_out)
    came_q = swap_tp(share_q, 1)
    cross_q = swap_in_slab(came_q, 1, 0)
    came_kv = swap_tp(share_kv, 1)
    half_rows = head_dim // sp_count
    out_sent = lax.dynamic_slice(
        w_out, (sp_place * half_rows, (mine ^ 1) * quarter), (half_rows, quarter)
    )
    out_came = swap_tp(out_sent, 1)
    out_other = swap_sp(out_came)
    weights = [w_query, w_kv, came_kv, swap_sp(came_kv), came_q, cross_q]
    weights += [swap_sp(came_q), swap_sp(cross_q)]
    early = call(
        early_kernel, [((len(firsts) * rows, 4 * head_dim), jnp.float32)], flags, firsts + weights
    )[0]

    in_order = lambda a, b, flag: [jnp.where(flag, a, b), jnp.where(flag, b, a)]
    low, high = in_order(out_came, out_other, sp_place == 0)
    out_pair = jnp.concatenate([low, high], axis=0)
    out_kept = lax.dynamic_slice_in_dim(w_out, mine * quarter, quarter, 1)
    out_own = jnp.concatenate(in_order(out_kept, out_pair, side == 0), axis=0)
    if short:
        out_first = swap_by_core(out_own, (2, 4))
        out_swapped = swap_sp(out_first)

    doc_ends = jnp.cumsum(doc_lengths)
    count = slabs * rows

    def place_of(index, flip_side, flip_core):
        at = (slab ^ (index // rows)) * 2 + (side ^ flip_side)
        return (at * sp_count + (sp_place ^ flip_core)) * rows + index % rows

    table = lambda shape, axis: lax.broadcasted_iota(jnp.int32, shape, axis)
    lane = table((count, head_dim), 1)
    row_places = place_of(table((count, head_dim), 0), 0, 0)
    half_head = head_dim // 2
    powers = (lane % half_head).astype(jnp.float32) * (2.0 / head_dim)
    angles = row_places.astype(jnp.float32) * jnp.power(10000.0, -powers)
    cosine = jnp.cos(angles)
    sine_part = jnp.where(lane < half_head, -jnp.sin(angles), jnp.sin(angles))
    places = place_of(jnp.arange(count, dtype=jnp.int32), 0, 0)
    ends = jnp.where(doc_ends[None, :] <= places[:, None], doc_ends[None, :], 0)
    starts = jnp.max(ends, axis=1)
    key_index = table((count, 4 * count), 1)
    key_places = place_of(key_index % count, key_index // count % 2, key_index // count // 2)
    query_places = place_of(table((count, 4 * count), 0), 0, 0)
    allowed = (key_places <= query_places) & (key_places >= starts[:, None])

    queries, key_value = call(
        tail_kernel,
        [((2 * count, head_dim), jnp.bfloat16), ((count, 2 * head_dim), jnp.bfloat16)],
        flags,
        [early, *last, cosine, sine_part] + weights,
        [pltpu.VMEM((rows, width), jnp.bfloat16)],
    )

    beside = swap_tp(key_value, 1)
    every = [key_value, beside, swap_sp(key_value), swap_sp(beside)]
    every = jnp.concatenate(every, axis=0)
    allowed = jnp.concatenate([allowed, allowed], axis=0)
    scores = jnp.einsum(
        "qd,kd->qk", queries, every[:, :head_dim], preferred_element_type=jnp.float32
    )
    largest = jnp.max(jnp.where(allowed, scores, masked_low), axis=1, keepdims=True)
    e = jnp.where(allowed, jnp.exp(scores - largest), 0.0)
    denominator = jnp.sum(e, axis=1, keepdims=True)
    mixed = plain(e.astype(jnp.bfloat16), every[:, head_dim:])
    mixed = (mixed / denominator).astype(jnp.bfloat16)
    mixed = jnp.concatenate(in_order(mixed[:count], mixed[count:], side == 0), axis=1)

    parts = [mixed[:rows]]
    for k in range(1, slabs):
        parts.append(swap_tp(mixed[k * rows : (k + 1) * rows], 2 * k))
    if short:
        parts[1:3] = in_order(parts[1], parts[2], sp_place == 0)
    merged = jnp.concatenate(parts, axis=1)
    peers = ((0, 0), (0, 1), (1, 0), (1, 1))
    stacked = [merged] + [swap_in_slab(merged, g, t) for g, t in peers[1:]]
    if short:
        out_sent = jnp.where(sp_place == 1, out_first, out_own)
        out_last = swap_by_core(out_sent, (6, 2), is_inner)
        out_last, stacked[2] = fence(out_last, stacked[2])
        pieces = [out_own, out_first, out_swapped, out_last, swap_sp(out_last)]
    else:
        pieces = [out_own]
        mine_of = lax.dynamic_slice_in_dim(out_own, sp_place * head_dim, head_dim, 0)
        for k in range(1, slabs):
            piece = swap_tp(mine_of, 2 * k)
            both = in_order(piece, swap_sp(piece), sp_place == 0)
            pieces.append(jnp.concatenate(both, axis=0))
    outs = call(
        lambda *refs: project_kernel(len(peers), short, *refs),
        [((rows, quarter), jnp.bfloat16)] * len(peers),
        flags,
        stacked + pieces,
    )
    outs = [outs[0]] + [swap_in_slab(o, g, t) for o, (g, t) in zip(outs[1:], peers[1:])]
    sems = [pltpu.SemaphoreType.DMA((len(outs),))]
    shape = ((rows, width), jnp.bfloat16)
    return call(assemble_kernel, [shape], flags, outs, sems, pl.ANY)[0]


def solution(mesh):
    placed = (
        P(("groups", "tp", "sp"), None),
        P(None, "tp"),
        P(None, "tp"),
        P(None, "tp"),
        P("tp", None),
        P("groups"),
    )

    return jax.shard_map(
        local,
        mesh=mesh,
        in_specs=placed,
        out_specs=P(("groups", "tp", "sp"), None),
        check_vma=False,
    )
```

time: 104 us -> 106 us (1.019)
  waiting for transfers between devices: 29.2 us -> 48.2 us
  starting transfers between devices: 46 us -> 32.8 us
  local copies, waits for them, and re-layouts: 5.84 us -> 3.47 us
  blocking collectives: 2.09 us -> 0 us
    ppermute x14 -> x11, starting transfers between devices: 30.9 us -> 17.4 us  [swap_tp(): return lax.ppermute(block, 'tp', route)]
    ppermute x14 -> x11, waiting for transfers between devices: 17.2 us -> 25.1 us  [swap_tp(): return lax.ppermute(block, 'tp', route)]
    ppermute x7, waiting for transfers between devices: 11.9 us -> 17.3 us  [swap_in_slab(): return lax.ppermute(block, ('groups', 'tp'), route)]
    select_n x3 -> x6, other arithmetic: 1.08 us -> 4.39 us  [the longest x4 2.03 us: local(): in_order = lambda a, b, flag: [jnp.where(flag, a, b), jnp.where(flag, b, a)]]
    ppermute x1 -> x2, waiting for transfers between devices: 0.01 us -> 3.26 us  [swap_by_core(): return lax.ppermute(block, ('tp', 'sp'), route)]
    ppermute x7 -> x8, starting transfers between devices: 1.32 us -> 4.38 us  [swap_sp(): return lax.ppermute(block, 'sp', [(s, s ^ 1) for s in range(count)])]
    add x5 -> x0, local copies, waits for them, and re-layouts: 2.89 us -> none  [places_of(): return (starts[:, None] + row_ids[None, :]).reshape(-1)]
    ppermute x1 -> x2, starting transfers between devices: 4.13 us -> 1.28 us  [swap_by_core(): return lax.ppermute(block, ('tp', 'sp'), route)]
  transfers between devices with their start and end apart: 29 -> 28, of which waited for: 9 -> 15; matrix products, arithmetic and copies ran while one was open for 13% -> 15% of each run, Pallas kernels for 5% -> 5%
where the time goes in v2:
time: 106 us
  waiting for transfers between devices  48.2 us (45%)
  starting transfers between devices  32.8 us (31%)
  other arithmetic  11.4 us (11%)
  Pallas kernels  8.85 us (8%)
  local copies, waits for them, and re-layouts  3.47 us (3%)
    ppermute x11, waiting for transfers between devices, swap_tp(): return lax.ppermute(block, 'tp', route)  25.1 us
    ppermute x11, starting transfers between devices, swap_tp(): return lax.ppermute(block, 'tp', route)  17.4 us
    ppermute x7, waiting for transfers between devices, swap_in_slab(): return lax.ppermute(block, ('groups', 'tp'), route)  17.3 us
    ppermute x7, starting transfers between devices, swap_in_slab(): return lax.ppermute(block, ('groups', 'tp'), route)  9.73 us
    pallas_call x4, Pallas kernels, call(): pl.pallas_call(kernel, in_specs=[pl.BlockSpec(memory_space=pltpu.SMEM)] +...  8.85 us
    ppermute x8, starting transfers between devices, swap_sp(): return lax.ppermute(block, 'sp', [(s, s ^ 1) for s in range(count)])  4.38 us
    ppermute x2, waiting for transfers between devices, swap_by_core(): return lax.ppermute(block, ('tp', 'sp'), route)  3.26 us
    ppermute x8, waiting for transfers between devices, swap_sp(): return lax.ppermute(block, 'sp', [(s, s ^ 1) for s in range(count)])  2.54 us
  transfers between devices with their start and end apart: 28, of which 15 were waited for; matrix products, arithmetic and copies ran while one was open for 15% of the time, Pallas kernels for 5%

profile of v2, /device:TPU:0, one launch (start us, length us, event | category | flops | bytes accessed | tf_op | source)
XLA Modules:
  0.0 105.9 jit_solution(2924061148782762809)
XLA Ops:
  0.0 3.1 %collective-permute-start = (bf16[48,4608]{1,0:T(8,128)(2,1)}, bf16[48,4608]{1,0:T(8,128)(2,1)}, u32[]{:S(2)}, u32[]{:S(2)}) collective-permute-start(bf16[48,4608]{1,0:T(8,128)(2,1)} %refs_0_.2), channel_id=1, source_target_pairs={{0,4},{2,6},{4,0},{6,2},{8,12},{10,14},{12,8},{14,10},{1,5},{3,7},... | collective-permute-start | bytes 1327112 | tf_op jit(solution)/shard_map/ppermute | solution.py:16
  3.1 2.6 %collective-permute-start.1 = (bf16[48,4608]{1,0:T(8,128)(2,1)}, bf16[48,4608]{1,0:T(8,128)(2,1)}, u32[]{:S(2)}, u32[]{:S(2)}) collective-permute-start(bf16[48,4608]{1,0:T(8,128)(2,1)} %refs_0_.2), channel_id=1, source_target_pairs={{0,8},{2,10},{4,12},{6,14},{8,0},{10,2},{12,4},{14,6},{1,9},{3,11}... | collective-permute-start | bytes 1327112 | tf_op jit(solution)/shard_map/ppermute | solution.py:16
  5.6 1.7 %constant_dynamic-slice_fusion = bf16[1152,128]{1,0:T(8,128)(2,1)} fusion(bf16[4608,128]{1,0:T(8,128)(2,1)} %refs_0_.3, s32[]{:T(128)S(6)} %select_n.184), kind=kLoop, calls=%fused_computation.99 | loop fusion | bytes 589828 | tf_op jit(solution)/shard_map/dynamic_slice | solution.py:188
  8.5 1.6 %collective-permute-start.2 = (bf16[128,2304]{1,0:T(8,128)(2,1)S(1)}, bf16[128,2304]{1,0:T(8,128)(2,1)S(1)}, u32[]{:S(2)}, u32[]{:S(2)}) collective-permute-start(bf16[128,2304]{1,0:T(8,128)(2,1)S(1)} %fusion.17), channel_id=1, source_target_pairs={{0,2},{2,0},{4,6},{6,4},{8,10},{10,8},{12,14},{14,12},{1,3},{3,1},... | collective-permute-start | bytes 1769480 | tf_op jit(solution)/shard_map/ppermute | solution.py:16
  10.6 1.6 %dynamic_slice.15 = bf16[64,1152]{1,0:T(8,128)(2,1)} dynamic-slice(bf16[128,4608]{1,0:T(8,128)(2,1)} %param.10, s32[]{:T(128)S(6)} %select_n.204, s32[]{:T(128)S(6)} %select_n.205), dynamic_slice_sizes={64,1152} | dynamic-slice | bytes 294916 | tf_op jit(solution)/shard_map/dynamic_slice | solution.py:197
  16.7 16.0 %collective-permute-done.17 = bf16[64,1152]{1,0:T(8,128)(2,1)} collective-permute-done((bf16[64,1152]{1,0:T(8,128)(2,1)}, bf16[64,1152]{1,0:T(8,128)(2,1)}, u32[]{:S(2)}, u32[]{:S(2)}) %collective-permute-start.17) | collective-permute-done | bytes 147488 | tf_op jit(solution)/shard_map/ppermute | solution.py:16
  43.2 4.8 %collective-permute-done.5.refs_8_.refs_5_ = bf16[1152,128]{1,0:T(8,128)(2,1)} collective-permute-done((bf16[1152,128]{1,0:T(8,128)(2,1)}, bf16[1152,128]{1,0:T(8,128)(2,1)}, u32[]{:S(2)}, u32[]{:S(2)}) %collective-permute-start.5) | collective-permute-done | bytes 294944 | tf_op jit(solution)/shard_map/ppermute | solution.py:43
  49.3 3.3 %collective-permute-done.19.refs_6_ = bf16[256,1152]{1,0:T(8,128)(2,1)} collective-permute-done((bf16[256,1152]{1,0:T(8,128)(2,1)}, bf16[256,1152]{1,0:T(8,128)(2,1)}, u32[]{:S(2)}, u32[]{:S(2)}) %collective-permute-start.19) | collective-permute-done | bytes 589856 | tf_op jit(solution)/shard_map/ppermute | solution.py:32
  52.5 3.7 %collective-permute-start.7 = (bf16[1152,128]{1,0:T(8,128)(2,1)}, bf16[1152,128]{1,0:T(8,128)(2,1)S(1)}, u32[]{:S(2)}, u32[]{:S(2)}) collective-permute-start(bf16[1152,128]{1,0:T(8,128)(2,1)} %collective-permute-done.5.refs_8_.refs_5_), channel_id=1, source_target_pairs={{0,1},{1,0},{2,3},{3,2},{4,5},{5,4},{6,7},{7,6},{8,9},{9,8},{10,11... | collective-permute-start | bytes 884744 | tf_op jit(solution)/shard_map/ppermute | solution.py:21
  58.4 2.9 %shard_map.64.early = f32[144,512]{1,0:T(8,128)S(1)} custom-call(s32[5]{0:T(128)S(1)} %stack.27.flags.refs_0_, bf16[48,4608]{1,0:T(8,128)(2,1)S(1)} %copy-done.1, bf16[48,4608]{1,0:T(8,128)(2,1)} %collective-permute-done.refs_1_, bf16[48,4608]{1,0:T(8,128)(2,1)} %collective-permute-done.1.refs_2_, bf16[4608,128]{1,0:T(8,128)(2,1)S(1)} %copy-done, ...), custom_call_target="tpu_custom_call" | custom-call | tf_op jit(solution)/shard_map/pallas_call | solution.py:57
  61.3 2.8 %collective-permute-done.9.relayed = bf16[48,4608]{1,0:T(8,128)(2,1)S(1)} collective-permute-done((bf16[48,4608]{1,0:T(8,128)(2,1)}, bf16[48,4608]{1,0:T(8,128)(2,1)S(1)}, u32[]{:S(2)}, u32[]{:S(2)}) %collective-permute-start.9) | collective-permute-done | bytes 442400 | tf_op jit(solution)/shard_map/ppermute | solution.py:16
  64.2 2.5 %shard_map.65 = (bf16[384,128]{1,0:T(8,128)(2,1)S(1)}, bf16[192,256]{1,0:T(8,128)(2,1)S(1)}) custom-call(s32[5]{0:T(128)S(1)} %stack.27.flags.refs_0_, f32[144,512]{1,0:T(8,128)S(1)} %shard_map.64.early, bf16[48,4608]{1,0:T(8,128)(2,1)S(1)} %collective-permute-done.8.middle, bf16[48,4608]{1,0:T(8,128)(2,1)S(1)} %collective-permute-done.9.relayed, ...), custom_call_target="tpu_custom_call" | custom-call | tf_op jit(solution)/shard_map/pallas_call | solution.py:57
  66.7 1.6 %collective-permute-start.10 = (bf16[192,256]{1,0:T(8,128)(2,1)S(1)}, bf16[192,256]{1,0:T(8,128)(2,1)S(1)}, u32[]{:S(2)}, u32[]{:S(2)}) collective-permute-start(bf16[192,256]{1,0:T(8,128)(2,1)S(1)} %get-tuple-element.21), channel_id=1, source_target_pairs={{0,2},{2,0},{4,6},{6,4},{8,10},{10,8},{12,14},{14,12},{1,3},{3,1},... | collective-permute-start | bytes 294920 | tf_op jit(solution)/shard_map/ppermute | solution.py:16
  68.3 3.1 %collective-permute-done.10 = bf16[192,256]{1,0:T(8,128)(2,1)S(1)} collective-permute-done((bf16[192,256]{1,0:T(8,128)(2,1)S(1)}, bf16[192,256]{1,0:T(8,128)(2,1)S(1)}, u32[]{:S(2)}, u32[]{:S(2)}) %collective-permute-start.10) | collective-permute-done | bytes 98336 | tf_op jit(solution)/shard_map/ppermute | solution.py:16
  76.1 2.4 %collective-permute-start.15 = (bf16[48,256]{1,0:T(8,128)(2,1)S(1)}, bf16[48,256]{1,0:T(8,128)(2,1)S(1)}, u32[]{:S(2)}, u32[]{:S(2)}) collective-permute-start(bf16[48,256]{1,0:T(8,128)(2,1)S(1)} %get-tuple-element.35), channel_id=1, source_target_pairs={{0,12},{2,14},{4,8},{6,10},{8,4},{10,6},{12,0},{14,2},{1,13},{3,15... | collective-permute-start | bytes 73736 | tf_op jit(solution)/shard_map/ppermute | solution.py:16
  79.4 2.3 %collective-permute-done.15 = bf16[48,256]{1,0:T(8,128)(2,1)S(1)} collective-permute-done((bf16[48,256]{1,0:T(8,128)(2,1)S(1)}, bf16[48,256]{1,0:T(8,128)(2,1)S(1)}, u32[]{:S(2)}, u32[]{:S(2)}) %collective-permute-start.15) | collective-permute-done | bytes 24608 | tf_op jit(solution)/shard_map/ppermute | solution.py:16
  81.7 1.6 %collective-permute-start.21 = (bf16[48,1024]{1,0:T(8,128)(2,1)S(1)}, bf16[48,1024]{1,0:T(8,128)(2,1)S(1)}, u32[]{:S(2)}, u32[]{:S(2)}) collective-permute-start(bf16[48,1024]{1,0:T(8,128)(2,1)S(1)} %pad_maximum_fusion.3.refs_1_), channel_id=1, source_target_pairs={{0,16},{2,18},{4,20},{6,22},{8,24},{10,26},{12,28},{14,30},{16,0},... | collective-permute-start | bytes 294920 | tf_op jit(solution)/shard_map/ppermute | solution.py:43
  83.3 3.0 %collective-permute-done.21.refs_3_ = bf16[48,1024]{1,0:T(8,128)(2,1)S(1)} collective-permute-done((bf16[48,1024]{1,0:T(8,128)(2,1)S(1)}, bf16[48,1024]{1,0:T(8,128)(2,1)S(1)}, u32[]{:S(2)}, u32[]{:S(2)}) %collective-permute-start.21) | collective-permute-done | bytes 98336 | tf_op jit(solution)/shard_map/ppermute | solution.py:43
  89.4 3.3 %collective-permute-done.16.refs_2_ = bf16[48,1024]{1,0:T(8,128)(2,1)S(1)} collective-permute-done((bf16[48,1024]{1,0:T(8,128)(2,1)S(1)}, bf16[48,1024]{1,0:T(8,128)(2,1)S(1)}, u32[]{:S(2)}, u32[]{:S(2)}) %collective-permute-start.16) | collective-permute-done | bytes 98336 | tf_op jit(solution)/shard_map/ppermute | solution.py:43
  93.7 2.0 %shard_map.66 = (bf16[48,1152]{1,0:T(8,128)(2,1)S(1)}, bf16[48,1152]{1,0:T(8,128)(2,1)S(1)}, bf16[48,1152]{1,0:T(8,128)(2,1)S(1)}, bf16[48,1152]{1,0:T(8,128)(2,1)S(1)}) custom-call(s32[5]{0:T(128)S(1)} %stack.27.flags.refs_0_, bf16[48,1024]{1,0:T(8,128)(2,1)S(1)} %pad_maximum_fusion.3.refs_1_, bf16[48,1024]{1,0:T(8,128)(2,1)S(1)} %collective-permute-done.16.refs_2_, ...), custom_call_target="tpu_custom_call" | custom-call | tf_op jit(solution)/shard_map/pallas_call | solution.py:57
  95.8 1.6 %collective-permute-start.25 = (bf16[48,1152]{1,0:T(8,128)(2,1)S(1)}, bf16[48,1152]{1,0:T(8,128)(2,1)S(1)}, u32[]{:S(2)}, u32[]{:S(2)}) collective-permute-start(bf16[48,1152]{1,0:T(8,128)(2,1)S(1)} %get-tuple-element.26), channel_id=1, source_target_pairs={{0,2},{2,0},{4,6},{6,4},{8,10},{10,8},{12,14},{14,12},{16,18},{18,... | collective-permute-start | bytes 331784 | tf_op jit(solution)/shard_map/ppermute | solution.py:43
  97.3 1.6 %collective-permute-start.26 = (bf16[48,1152]{1,0:T(8,128)(2,1)S(1)}, bf16[48,1152]{1,0:T(8,128)(2,1)S(1)}, u32[]{:S(2)}, u32[]{:S(2)}) collective-permute-start(bf16[48,1152]{1,0:T(8,128)(2,1)S(1)} %get-tuple-element.27), channel_id=1, source_target_pairs={{0,16},{2,18},{4,20},{6,22},{8,24},{10,26},{12,28},{14,30},{16,0},... | collective-permute-start | bytes 331784 | tf_op jit(solution)/shard_map/ppermute | solution.py:43
  100.6 2.3 %collective-permute-done.26.refs_2_ = bf16[48,1152]{1,0:T(8,128)(2,1)S(1)} collective-permute-done((bf16[48,1152]{1,0:T(8,128)(2,1)S(1)}, bf16[48,1152]{1,0:T(8,128)(2,1)S(1)}, u32[]{:S(2)}, u32[]{:S(2)}) %collective-permute-start.26) | collective-permute-done | bytes 110624 | tf_op jit(solution)/shard_map/ppermute | solution.py:43
  102.9 1.7 %collective-permute-done.27.refs_3_ = bf16[48,1152]{1,0:T(8,128)(2,1)S(1)} collective-permute-done((bf16[48,1152]{1,0:T(8,128)(2,1)S(1)}, bf16[48,1152]{1,0:T(8,128)(2,1)S(1)}, u32[]{:S(2)}, u32[]{:S(2)}) %collective-permute-start.27) | collective-permute-done | bytes 110624 | tf_op jit(solution)/shard_map/ppermute | solution.py:43
  (107 shorter events, 32.5 us)
Async XLA Ops:
  0.0 41.8 %collective-permute-start = (bf16[48,4608]{1,0:T(8,128)(2,1)}, bf16[48,4608]{1,0:T(8,128)(2,1)}, u32[]{:S(2)}, u32[]{:S(2)}) collective-permute-start(bf16[48,4608]{1,0:T(8,128)(2,1)} %refs_0_.2), channel_id=1, source_target_pairs={{0,4},{2,6},{4,0},{6,2},{8,12},{10,14},{12,8},{14,10},{1,5},{3,7},... | collective-permute-start | bytes 1327112 | tf_op jit(solution)/shard_map/ppermute | solution.py:16
  3.1 39.6 %collective-permute-start.1 = (bf16[48,4608]{1,0:T(8,128)(2,1)}, bf16[48,4608]{1,0:T(8,128)(2,1)}, u32[]{:S(2)}, u32[]{:S(2)}) collective-permute-start(bf16[48,4608]{1,0:T(8,128)(2,1)} %refs_0_.2), channel_id=1, source_target_pairs={{0,8},{2,10},{4,12},{6,14},{8,0},{10,2},{12,4},{14,6},{1,9},{3,11}... | collective-permute-start | bytes 1327112 | tf_op jit(solution)/shard_map/ppermute | solution.py:16
  8.5 32.0 %collective-permute-start.2 = (bf16[128,2304]{1,0:T(8,128)(2,1)S(1)}, bf16[128,2304]{1,0:T(8,128)(2,1)S(1)}, u32[]{:S(2)}, u32[]{:S(2)}) collective-permute-start(bf16[128,2304]{1,0:T(8,128)(2,1)S(1)} %fusion.17), channel_id=1, source_target_pairs={{0,2},{2,0},{4,6},{6,4},{8,10},{10,8},{12,14},{14,12},{1,3},{3,1},... | collective-permute-start | bytes 1769480 | tf_op jit(solution)/shard_map/ppermute | solution.py:16
  10.1 28.9 %collective-permute-start.4 = (bf16[1152,128]{1,0:T(8,128)(2,1)}, bf16[1152,128]{1,0:T(8,128)(2,1)}, u32[]{:S(2)}, u32[]{:S(2)}) collective-permute-start(bf16[1152,128]{1,0:T(8,128)(2,1)} %constant_dynamic-slice_fusion), channel_id=1, source_target_pairs={{0,2},{2,0},{4,6},{6,4},{8,10},{10,8},{12,14},{14,12},{1,3},{3,1},... | collective-permute-start | bytes 884744 | tf_op jit(solution)/shard_map/ppermute | solution.py:16
  12.2 20.5 %collective-permute-start.17 = (bf16[64,1152]{1,0:T(8,128)(2,1)}, bf16[64,1152]{1,0:T(8,128)(2,1)}, u32[]{:S(2)}, u32[]{:S(2)}) collective-permute-start(bf16[64,1152]{1,0:T(8,128)(2,1)} %dynamic_slice.15), channel_id=1, source_target_pairs={{0,2},{2,0},{4,6},{6,4},{8,10},{10,8},{12,14},{14,12},{1,3},{3,1},... | collective-permute-start | bytes 442376 | tf_op jit(solution)/shard_map/ppermute | solution.py:16
  37.3 15.2 %collective-permute-start.19 = (bf16[256,1152]{1,0:T(8,128)(2,1)}, bf16[256,1152]{1,0:T(8,128)(2,1)}, u32[]{:S(2)}, u32[]{:S(2)}) collective-permute-start(bf16[256,1152]{1,0:T(8,128)(2,1)} %pad_maximum_fusion.1.refs_5_), channel_id=1, source_target_pairs={{0,4},{1,9},{2,6},{3,11},{4,0},{5,13},{6,2},{7,15},{8,12},{9,1},{1... | collective-permute-start | bytes 1769480 | tf_op jit(solution)/shard_map/ppermute | solution.py:32
  39.0 9.0 %collective-permute-start.5 = (bf16[1152,128]{1,0:T(8,128)(2,1)}, bf16[1152,128]{1,0:T(8,128)(2,1)}, u32[]{:S(2)}, u32[]{:S(2)}) collective-permute-start(bf16[1152,128]{1,0:T(8,128)(2,1)} %collective-permute-done.4.refs_7_.refs_4_), channel_id=1, source_target_pairs={{0,16},{2,18},{4,20},{6,22},{8,24},{10,26},{12,28},{14,30},{16,0},... | collective-permute-start | bytes 884744 | tf_op jit(solution)/shard_map/ppermute | solution.py:43
  40.5 17.9 %collective-permute-start.3 = (bf16[128,2304]{1,0:T(8,128)(2,1)S(1)}, bf16[128,2304]{1,0:T(8,128)(2,1)S(1)}, u32[]{:S(2)}, u32[]{:S(2)}) collective-permute-start(bf16[128,2304]{1,0:T(8,128)(2,1)S(1)} %collective-permute-done.2.refs_5_.refs_2_), channel_id=1, source_target_pairs={{0,1},{1,0},{2,3},{3,2},{4,5},{5,4},{6,7},{7,6},{8,9},{9,8},{10,11... | collective-permute-start | bytes 1769480 | tf_op jit(solution)/shard_map/ppermute | solution.py:21
  41.8 19.5 %collective-permute-start.8 = (bf16[48,4608]{1,0:T(8,128)(2,1)}, bf16[48,4608]{1,0:T(8,128)(2,1)S(1)}, u32[]{:S(2)}, u32[]{:S(2)}) collective-permute-start(bf16[48,4608]{1,0:T(8,128)(2,1)} %refs_0_.2), channel_id=1, source_target_pairs={{4,8},{6,10},{8,4},{10,6},{5,9},{7,11},{9,5},{11,7},{20,24},{22,26... | collective-permute-start | bytes 1327112 | tf_op jit(solution)/shard_map/ppermute | solution.py:16
  42.7 14.8 %collective-permute-start.6 = (bf16[1152,128]{1,0:T(8,128)(2,1)}, bf16[1152,128]{1,0:T(8,128)(2,1)S(1)}, u32[]{:S(2)}, u32[]{:S(2)}) collective-permute-start(bf16[1152,128]{1,0:T(8,128)(2,1)} %collective-permute-done.4.refs_7_.refs_4_), channel_id=1, source_target_pairs={{0,1},{1,0},{2,3},{3,2},{4,5},{5,4},{6,7},{7,6},{8,9},{9,8},{10,11... | collective-permute-start | bytes 884744 | tf_op jit(solution)/shard_map/ppermute | solution.py:21
  48.0 16.2 %collective-permute-start.9 = (bf16[48,4608]{1,0:T(8,128)(2,1)}, bf16[48,4608]{1,0:T(8,128)(2,1)S(1)}, u32[]{:S(2)}, u32[]{:S(2)}) collective-permute-start(bf16[48,4608]{1,0:T(8,128)(2,1)} %collective-permute-done.1.refs_2_), channel_id=1, source_target_pairs={{4,0},{6,2},{8,12},{10,14},{5,1},{7,3},{9,13},{11,15},{20,16},{22,... | collective-permute-start | bytes 1327112 | tf_op jit(solution)/shard_map/ppermute | solution.py:16
  52.5 5.8 %collective-permute-start.7 = (bf16[1152,128]{1,0:T(8,128)(2,1)}, bf16[1152,128]{1,0:T(8,128)(2,1)S(1)}, u32[]{:S(2)}, u32[]{:S(2)}) collective-permute-start(bf16[1152,128]{1,0:T(8,128)(2,1)} %collective-permute-done.5.refs_8_.refs_5_), channel_id=1, source_target_pairs={{0,1},{1,0},{2,3},{3,2},{4,5},{5,4},{6,7},{7,6},{8,9},{9,8},{10,11... | collective-permute-start | bytes 884744 | tf_op jit(solution)/shard_map/ppermute | solution.py:21
  57.5 25.8 %collective-permute-start.20 = (bf16[256,1152]{1,0:T(8,128)(2,1)S(1)}, bf16[256,1152]{1,0:T(8,128)(2,1)S(1)}, u32[]{:S(2)}, u32[]{:S(2)}) collective-permute-start(bf16[256,1152]{1,0:T(8,128)(2,1)S(1)} %broadcast_select_fusion), channel_id=1, source_target_pairs={{4,8},{5,1},{6,10},{7,3},{8,4},{9,13},{10,6},{11,15},{20,24},{21,1... | collective-permute-start | bytes 1769480 | tf_op jit(solution)/shard_map/ppermute | solution.py:32
  66.7 4.7 %collective-permute-start.10 = (bf16[192,256]{1,0:T(8,128)(2,1)S(1)}, bf16[192,256]{1,0:T(8,128)(2,1)S(1)}, u32[]{:S(2)}, u32[]{:S(2)}) collective-permute-start(bf16[192,256]{1,0:T(8,128)(2,1)S(1)} %get-tuple-element.21), channel_id=1, source_target_pairs={{0,2},{2,0},{4,6},{6,4},{8,10},{10,8},{12,14},{14,12},{1,3},{3,1},... | collective-permute-start | bytes 294920 | tf_op jit(solution)/shard_map/ppermute | solution.py:16
  74.6 4.8 %collective-permute-start.14 = (bf16[48,256]{1,0:T(8,128)(2,1)S(1)}, bf16[48,256]{1,0:T(8,128)(2,1)S(1)}, u32[]{:S(2)}, u32[]{:S(2)}) collective-permute-start(bf16[48,256]{1,0:T(8,128)(2,1)S(1)} %get-tuple-element.36), channel_id=1, source_target_pairs={{0,8},{2,10},{4,12},{6,14},{8,0},{10,2},{12,4},{14,6},{1,9},{3,11}... | collective-permute-start | bytes 73736 | tf_op jit(solution)/shard_map/ppermute | solution.py:16
  76.1 5.6 %collective-permute-start.15 = (bf16[48,256]{1,0:T(8,128)(2,1)S(1)}, bf16[48,256]{1,0:T(8,128)(2,1)S(1)}, u32[]{:S(2)}, u32[]{:S(2)}) collective-permute-start(bf16[48,256]{1,0:T(8,128)(2,1)S(1)} %get-tuple-element.35), channel_id=1, source_target_pairs={{0,12},{2,14},{4,8},{6,10},{8,4},{10,6},{12,0},{14,2},{1,13},{3,15... | collective-permute-start | bytes 73736 | tf_op jit(solution)/shard_map/ppermute | solution.py:16
  81.7 4.7 %collective-permute-start.21 = (bf16[48,1024]{1,0:T(8,128)(2,1)S(1)}, bf16[48,1024]{1,0:T(8,128)(2,1)S(1)}, u32[]{:S(2)}, u32[]{:S(2)}) collective-permute-start(bf16[48,1024]{1,0:T(8,128)(2,1)S(1)} %pad_maximum_fusion.3.refs_1_), channel_id=1, source_target_pairs={{0,16},{2,18},{4,20},{6,22},{8,24},{10,26},{12,28},{14,30},{16,0},... | collective-permute-start | bytes 294920 | tf_op jit(solution)/shard_map/ppermute | solution.py:43
  83.3 6.1 %collective-permute-start.23 = (bf16[256,1152]{1,0:T(8,128)(2,1)}, bf16[256,1152]{1,0:T(8,128)(2,1)S(1)}, u32[]{:S(2)}, u32[]{:S(2)}) collective-permute-start(bf16[256,1152]{1,0:T(8,128)(2,1)} %collective-permute-done.19.refs_6_), channel_id=1, source_target_pairs={{0,1},{1,0},{2,3},{3,2},{4,5},{5,4},{6,7},{7,6},{8,9},{9,8},{10,11... | collective-permute-start | bytes 1769480 | tf_op jit(solution)/shard_map/ppermute | solution.py:21
  86.4 7.4 %collective-permute-start.24 = (bf16[256,1152]{1,0:T(8,128)(2,1)S(1)}, bf16[256,1152]{1,0:T(8,128)(2,1)S(1)}, u32[]{:S(2)}, u32[]{:S(2)}) collective-permute-start(bf16[256,1152]{1,0:T(8,128)(2,1)S(1)} %collective-permute-done.20.refs_8_), channel_id=1, source_target_pairs={{0,1},{1,0},{2,3},{3,2},{4,5},{5,4},{6,7},{7,6},{8,9},{9,8},{10,11... | collective-permute-start | bytes 1769480 | tf_op jit(solution)/shard_map/ppermute | solution.py:21
  86.4 6.4 %collective-permute-start.16 = (bf16[48,1024]{1,0:T(8,128)(2,1)S(1)}, bf16[48,1024]{1,0:T(8,128)(2,1)S(1)}, u32[]{:S(2)}, u32[]{:S(2)}) collective-permute-start(bf16[48,1024]{1,0:T(8,128)(2,1)S(1)} %pad_maximum_fusion.3.refs_1_), channel_id=1, source_target_pairs={{0,2},{2,0},{4,6},{6,4},{8,10},{10,8},{12,14},{14,12},{16,18},{18,... | collective-permute-start | bytes 294920 | tf_op jit(solution)/shard_map/ppermute | solution.py:43
  87.9 5.8 %collective-permute-start.22 = (bf16[48,1024]{1,0:T(8,128)(2,1)S(1)}, bf16[48,1024]{1,0:T(8,128)(2,1)S(1)}, u32[]{:S(2)}, u32[]{:S(2)}) collective-permute-start(bf16[48,1024]{1,0:T(8,128)(2,1)S(1)} %pad_maximum_fusion.3.refs_1_), channel_id=1, source_target_pairs={{0,18},{2,16},{4,22},{6,20},{8,26},{10,24},{12,30},{14,28},{16,2},... | collective-permute-start | bytes 294920 | tf_op jit(solution)/shard_map/ppermute | solution.py:43
  95.8 4.8 %collective-permute-start.25 = (bf16[48,1152]{1,0:T(8,128)(2,1)S(1)}, bf16[48,1152]{1,0:T(8,128)(2,1)S(1)}, u32[]{:S(2)}, u32[]{:S(2)}) collective-permute-start(bf16[48,1152]{1,0:T(8,128)(2,1)S(1)} %get-tuple-element.26), channel_id=1, source_target_pairs={{0,2},{2,0},{4,6},{6,4},{8,10},{10,8},{12,14},{14,12},{16,18},{18,... | collective-permute-start | bytes 331784 | tf_op jit(solution)/shard_map/ppermute | solution.py:43
  97.3 5.5 %collective-permute-start.26 = (bf16[48,1152]{1,0:T(8,128)(2,1)S(1)}, bf16[48,1152]{1,0:T(8,128)(2,1)S(1)}, u32[]{:S(2)}, u32[]{:S(2)}) collective-permute-start(bf16[48,1152]{1,0:T(8,128)(2,1)S(1)} %get-tuple-element.27), channel_id=1, source_target_pairs={{0,16},{2,18},{4,20},{6,22},{8,24},{10,26},{12,28},{14,30},{16,0},... | collective-permute-start | bytes 331784 | tf_op jit(solution)/shard_map/ppermute | solution.py:43
  98.9 5.6 %collective-permute-start.27 = (bf16[48,1152]{1,0:T(8,128)(2,1)S(1)}, bf16[48,1152]{1,0:T(8,128)(2,1)S(1)}, u32[]{:S(2)}, u32[]{:S(2)}) collective-permute-start(bf16[48,1152]{1,0:T(8,128)(2,1)S(1)} %get-tuple-element.28), channel_id=1, source_target_pairs={{0,18},{2,16},{4,22},{6,20},{8,26},{10,24},{12,30},{14,28},{16,2},... | collective-permute-start | bytes 331784 | tf_op jit(solution)/shard_map/ppermute | solution.py:43
  (23 other events, 134.7 us)
